TPU v7x, 32 devices: a whole 2x2x4 slice. The times are simulated.
32 devices in a mesh: expert: 8 (over z, y), mp: 4 (over x, core).
Axes of the slice: x: 2, y: 2, z: 4, core: 2. Of those that a mesh axis runs over, the one named last changes fastest.
Arguments:
- queries: bfloat16 [256, 48, 128], P('expert', 'mp'), may hold values from -140 to 140
- k_cache: bfloat16 [256, 8, 128, 128], P('expert', 'mp'), may hold values from -5 to 5
- v_cache: bfloat16 [256, 8, 128, 128], P('expert', 'mp'), may hold values from -6 to 6
- lengths: int32 [256], P('expert'), may hold values from 2 to 128
- moe_input: bfloat16 [256, 6144], P('expert', 'mp'), may hold values from -40 to 40
- norm_gain: float32 [6144], P('mp'), may hold values from 0.5 to 1.5
- expert_ids: int32 [256, 2], P('expert'), may hold values from 0 to 7, all different within a row; in each aligned block of 32 rows (0 to 31, 32 to 63, ...) at most 16 rows name the same one
- combine_weights: float32 [256, 2], P('expert'), may hold values from 0.1 to 1
- capacity: int32 [8], replicated, may hold values from 8 to 16
- w_gate: bfloat16 [8, 6144, 8192], P('expert', None, 'mp'), may hold values from -0.078125 to 0.078125
- w_up: bfloat16 [8, 6144, 8192], P('expert', None, 'mp'), may hold values from -0.078125 to 0.078125
- w_down: bfloat16 [8, 8192, 6144], P('expert', 'mp'), may hold values from -0.0625 to 0.0625
Outputs:
- context: bfloat16 [256, 48, 128], P('expert', 'mp')
- layer_out: bfloat16 [256, 6144], P('expert', 'mp')
Inputs may be any that keep to these rules, and one draw needn't show every extreme that they name: `expert_ids`: within each aligned block of 32 tokens, no expert is named by more than 16 tokens; the 2 ids of a token differ.
All inputs are finite; a program needn't handle non-finite values.
Results may differ from a plain program's by a relative error of at most 0.007.
Values may be sent and summed in bfloat16 or wider, within the bound.
No kernel may reach another device: no remote copies, remote signals or barrier semaphores. Data moves between devices by JAX's collectives and lax.ppermute only.
A program may use at most 128 MiB of HBM per device.

v0:
```python
import functools

import jax
import jax.numpy as jnp
from jax import lax
from jax.experimental import pallas as pl
from jax.experimental.pallas import tpu as pltpu
from jax.sharding import PartitionSpec as P


TOP = 2
WIDE = 512
DEEP = 256
EARLY = 6
LATER = 3
VMEM_ROWS = 128
ROUTE_FLOPS = 2e10
PACK_FLOPS = 2e10


IN_VMEM = pl.BlockSpec(memory_space=pltpu.VMEM)
IN_PLACE = pl.BlockSpec(memory_space=pl.ANY)


def attention(queries, k_cache, v_cache, lengths):
    seq_count, head_count, head_size = queries.shape
    kv_count = k_cache.shape[1]
    group_size = head_count // kv_count
    queries_grouped = queries.reshape(seq_count, kv_count, group_size, head_size)
    scores = jnp.einsum(
        "bjgd,bjpd->bjgp", queries_grouped, k_cache, preferred_element_type=jnp.float32
    ) * head_size ** (-0.5)
    positions = jnp.arange(k_cache.shape[2])
    live_mask = positions[None, :] < lengths[:, None]
    scores = jnp.where(live_mask[:, None, None, :], scores, -jnp.inf)
    top_score = jnp.max(scores, axis=-1, keepdims=True)
    expo = jnp.exp(scores - top_score)
    probs = (expo / jnp.sum(expo, axis=-1, keepdims=True)).astype(jnp.bfloat16)
    context = jnp.einsum("bjgp,bjpd->bjgd", probs, v_cache, preferred_element_type=jnp.float32)
    return context.astype(jnp.bfloat16).reshape(seq_count, head_count, head_size)


def attend_kernel(scale, seqs, lengths_at, q_at, k_at, v_at, out, lengths, q, k, v, wide, score, prob, sems):
    copies = [
        pltpu.make_async_copy(source, target, sems.at[i])
        for i, (source, target) in enumerate(
            ((lengths_at, lengths), (q_at, q), (k_at, k), (v_at, v))
        )
    ]
    for copy in copies:
        copy.start()
    heads, size = q.shape[0] // seqs, q.shape[1]
    kv = k.shape[1]
    tall = wide.shape[0] // seqs
    group = heads // kv
    positions = k.shape[2]
    row = lax.broadcasted_iota(jnp.int32, (tall, positions), 0)
    lane = lax.broadcasted_iota(jnp.int32, (tall, positions), 1)
    copies[0].wait()
    copies[1].wait()
    wide[: heads * seqs, :] = q[...].astype(jnp.float32)
    wide[heads * seqs :, :] = jnp.zeros(((tall - heads) * seqs, size), jnp.float32)
    copies[2].wait()
    for b in range(seqs):
        queries = wide[pl.ds(b, tall, stride=seqs), :].astype(jnp.bfloat16)
        total = None
        for j in range(kv):
            dots = lax.dot_general(
                queries,
                k[b, j],
                (((1,), (1,)), ((), ())),
                preferred_element_type=jnp.float32,
            )
            total = dots if total is None else jnp.where(row < j * group, total, dots)
        live = lane < lengths[b]
        score[b * tall : (b + 1) * tall, :] = jnp.where(live, total * scale, -jnp.inf)
    top = jnp.max(score[...], axis=-1, keepdims=True)
    expo = jnp.exp(score[...] - top)
    prob[...] = (expo / jnp.sum(expo, axis=-1, keepdims=True)).astype(jnp.bfloat16)
    copies[3].wait()
    for b in range(seqs):
        probs = prob[b * tall : (b + 1) * tall, :].astype(jnp.float32)
        total = jnp.zeros((tall, size), jnp.float32)
        for j in range(kv):
            mine = (row >= j * group) & (row < (j + 1) * group)
            total = total + jnp.dot(
                jnp.where(mine, probs, 0.0).astype(jnp.bfloat16),
                v[b, j],
                preferred_element_type=jnp.float32,
            )
        wide[pl.ds(b, tall, stride=seqs), :] = total
    out[...] = wide[: heads * seqs, :].astype(jnp.bfloat16)


def position():
    member = lax.axis_index("mp")
    return member, member % 2, member // 2


def route_kernel(slots, split, ids_at, weights_at, cap_at, select, weighted, ids, weights, cap, sems):
    loads = [
        pltpu.make_async_copy(ids_at, ids, sems.at[0]),
        pltpu.make_async_copy(weights_at, weights, sems.at[1]),
        pltpu.make_async_copy(cap_at, cap, sems.at[2]),
    ]
    for load in loads:
        load.start()
    core, block = position()[1], lax.axis_index("expert")
    rows, tokens = select.shape
    row = lax.broadcasted_iota(jnp.int32, (rows, tokens), 0)
    step = row // slots
    slot = row - step * slots
    expert = jnp.bitwise_xor(block, 2 * step + core) // split
    before = lax.broadcasted_iota(jnp.int32, (tokens, tokens), 0)
    after = lax.broadcasted_iota(jnp.int32, (tokens, tokens), 1)
    earlier = (before < after).astype(jnp.float32)
    for load in loads:
        load.wait()
    first = ids[0:1, :] == expert
    named = first | (ids[1:2, :] == expert)
    rank = jnp.dot(named.astype(jnp.float32), earlier, preferred_element_type=jnp.float32)
    rank = rank.astype(jnp.int32)
    limit = jnp.zeros((rows, tokens), jnp.int32)
    for e in range(cap.shape[0]):
        limit = jnp.where(expert == e, cap[e], limit)
    chosen = named & (rank == slot) & (rank < limit)
    weighted[...] = jnp.where(
        chosen, jnp.where(first, weights[0:1, :], weights[1:2, :]), 0.0
    )
    select[...] = chosen.astype(jnp.float32).astype(jnp.bfloat16)


def pack_kernel(slots, first, width, select, *refs):
    sources, sends = refs[: width // refs[0].shape[1]], refs[width // refs[0].shape[1] :]
    member = position()[0]
    feat = sources[0].shape[1]
    rows = select[first * slots : (first + len(sends)) * slots, :]
    for i, source in enumerate(sources):
        moved = jnp.dot(rows, source[...], preferred_element_type=jnp.float32)
        moved = moved.astype(jnp.bfloat16)
        place = lax.rem(jnp.bitwise_xor(member, i) * feat, width)
        columns = pl.ds(pl.multiple_of(place, 128), feat)
        for k, send in enumerate(sends):
            send[:, columns] = moved[k * slots : (k + 1) * slots, :]


def gain_kernel(own, sibling, across, both, out):
    member = position()[0]
    feat = own.shape[1]
    for i, part in enumerate((own, sibling, across, both)):
        place = jnp.bitwise_xor(member, i)
        out[:, pl.ds(pl.multiple_of(place * feat, 128), feat)] = part[...]


def norm_kernel(*refs):
    parts, (gain, out) = refs[:-2], refs[-2:]
    plane = position()[2]
    width, depth = parts[0].shape[1], out.shape[1]
    starts = (plane * width, (1 - plane) * width) if len(parts) == 2 else (0,)
    total = jnp.zeros((out.shape[0], 128), jnp.float32)
    for part in parts:
        for j in range(width // 128):
            v = part[:, j * 128 : (j + 1) * 128].astype(jnp.float32)
            total = total + v * v
    mean = jnp.sum(total, axis=1, keepdims=True) / depth
    scale = lax.rsqrt(mean + 1e-05)
    for part, start in zip(parts, starts):
        for j in range(0, width, WIDE):
            columns = pl.ds(pl.multiple_of(start + j, 128), WIDE)
            v = part[:, j : j + WIDE].astype(jnp.float32)
            out[:, columns] = (v * scale * gain[:, columns]).astype(jnp.bfloat16)


def half_load(w_down, target, sems, first):
    width = w_down.shape[1] // 2
    blocks = w_down.shape[0] // DEEP
    plane = position()[2]

    def load(i):
        half, block = divmod(first + i, blocks)
        start = (plane if half else 1 - plane) * width
        return pltpu.make_async_copy(
            w_down.at[block * DEEP : (block + 1) * DEEP, pl.ds(pl.multiple_of(start, 128), width)],
            target.at[i * DEEP : (i + 1) * DEEP, :],
            sems.at[i],
        )

    return load


def hidden_kernel(count, *refs):
    rows_in, (w_gate, w_up, w_down, hidden, ahead, sems) = refs[:count], refs[count:]
    load = half_load(w_down, ahead, sems, 0)
    blocks = sems.shape[0]
    for i in range(blocks):
        load(i).start()

    @pl.loop(0, w_gate.shape[1] // WIDE)
    def _(j):
        columns = pl.ds(pl.multiple_of(j * WIDE, WIDE), WIDE)
        rows = jnp.concatenate([r[...] for r in rows_in], axis=0)
        gate = jnp.dot(rows, w_gate[:, columns], preferred_element_type=jnp.float32)
        up = jnp.dot(rows, w_up[:, columns], preferred_element_type=jnp.float32)
        hidden[:, columns] = (gate / (1.0 + jnp.exp(-gate)) * up).astype(jnp.bfloat16)

    for i in range(blocks):
        load(i).wait()


def down_kernel(first, later, hidden, ready, w_down, own, sib, *refs):
    if later:
        ahead, here, total, sems, sems_later = refs
    else:
        here, total, sems = refs
    half, width = own.shape
    known, missing = ready.shape[0], sems.shape[0]
    load = half_load(w_down, here, sems, first + known // DEEP)
    for i in range(missing):
        load(i).start()
    if later:
        load_later = half_load(w_down, ahead, sems_later, first + known // DEEP + missing)
        for i in range(later):
            load_later(i).start()
    for step in range(missing + 1):
        if step == 0:
            left, weight = hidden.at[:, :known], ready
        else:
            load(step - 1).wait()
            at = known + (step - 1) * DEEP
            left = hidden.at[:, at : at + DEEP]
            weight = here.at[(step - 1) * DEEP : step * DEEP, :]
        for j in range(width // WIDE):
            columns = slice(j * WIDE, (j + 1) * WIDE)
            out = jnp.dot(left[...], weight[:, columns], preferred_element_type=jnp.float32)
            if step > 0:
                out = out + total[:, columns]
            if step < missing:
                total[:, columns] = out
            else:
                own[:, columns] = out[:half, :]
                sib[:, columns] = out[half:, :].astype(jnp.bfloat16)
    if later:
        for i in range(later):
            load_later(i).wait()


def merge_kernel(own, arrived, *sends):
    slots = sends[0].shape[0]
    for k, send in enumerate(sends):
        at = slice(k * slots, (k + 1) * slots)
        send[...] = (own[at, :] + arrived[at, :].astype(jnp.float32)).astype(jnp.bfloat16)


def fold_kernel(k, own, arrived, crossed, out):
    slots = out.shape[0]
    at = slice(k * slots, (k + 1) * slots)
    total = own[at, :] + arrived[at, :].astype(jnp.float32)
    out[...] = (total + crossed[...].astype(jnp.float32)).astype(jnp.bfloat16)


def combine_kernel(rounds, weighted, residual, *refs):
    backs, (mine, send, total) = refs[:rounds], refs[rounds:]
    feat = residual.shape[1]
    core = position()[1]
    rows = jnp.concatenate([b[...].astype(jnp.float32) for b in backs], axis=0)
    total[...] = lax.dot_general(
        weighted[...],
        rows,
        (((0,), (0,)), ((), ())),
        precision=lax.Precision.HIGHEST,
        preferred_element_type=jnp.float32,
    )
    here = pl.ds(pl.multiple_of(core * feat, 128), feat)
    away = pl.ds(pl.multiple_of((1 - core) * feat, 128), feat)
    mine[...] = residual[...].astype(jnp.float32) + total[:, here]
    send[...] = total[:, away]


def held(*shape, dtype=jnp.bfloat16):
    return pltpu.VMEM(shape, dtype)


def in_vmem(v):
    return pltpu.with_memory_space_constraint(v, pltpu.VMEM)


def in_hbm(v):
    return pltpu.with_memory_space_constraint(v, pltpu.HBM)


def call(body, args, specs, outs, scratch=(), mib=2, flops=0, moved=0, alias=None):
    return pl.pallas_call(
        body,
        out_shape=outs,
        in_specs=specs,
        out_specs=[IN_VMEM] * len(outs),
        scratch_shapes=list(scratch),
        compiler_params=pltpu.CompilerParams(vmem_limit_bytes=mib << 20),
        cost_estimate=pl.CostEstimate(
            flops=int(flops), bytes_accessed=int(moved), transcendentals=0
        ),
        input_output_aliases=alias or {},
    )(*args)


def expert_layer(
    moe_input, norm_gain, expert_ids, combine_weights, capacity, w_gate, w_up, w_down
):
    devices, members = lax.axis_size("expert"), lax.axis_size("mp")
    tokens, feat = moe_input.shape
    split = devices // capacity.shape[0]
    slots = tokens // 2
    rounds = devices // 2
    rows = rounds * slots
    width, depth = 2 * feat, members * feat
    hid = w_gate.shape[2]
    order = range(rounds)
    f32 = jnp.float32

    def across(v, bit):
        return lax.ppermute(v, "mp", [(i, i ^ bit) for i in range(members)])

    def between(v, k):
        pairs = [
            (e * members + m, (e ^ (2 * k + m % 2)) * members + m)
            for e in range(devices)
            for m in range(members)
        ]
        return lax.ppermute(v, ("expert", "mp"), pairs)

    low = rounds // 2
    sibling = across(moe_input, 1)
    opposite = across(moe_input, 2)
    select, weighted = call(
        functools.partial(route_kernel, slots, split),
        [in_hbm(expert_ids.T), in_hbm(combine_weights.T), in_hbm(capacity)],
        [IN_PLACE] * 3,
        [held(rows, tokens), held(rows, tokens, dtype=f32)],
        scratch=[
            pltpu.VMEM((TOP, tokens), jnp.int32),
            pltpu.VMEM((TOP, tokens), f32),
            pltpu.SMEM(capacity.shape, jnp.int32),
            pltpu.SemaphoreType.DMA((3,)),
        ],
        flops=ROUTE_FLOPS,
        moved=1e5,
    )
    gain, sibling, select = lax.optimization_barrier((norm_gain[None, :], sibling, select))

    def pack(first, count, total, sources):
        return call(
            functools.partial(pack_kernel, slots, first, total),
            [select, *sources],
            [IN_VMEM] * (1 + len(sources)),
            [held(slots, total)] * count,
            flops=PACK_FLOPS,
            moved=1e6,
        )

    high_sends = pack(low, rounds - low, width, [moe_input, sibling])
    near = [between(high_sends[k - low], k) for k in range(low, rounds)]
    diagonal = across(opposite, 1)
    low_sends = pack(0, low, depth, [moe_input, sibling, opposite, diagonal])
    full = [between(low_sends[k], k) for k in range(low)]

    gain, _ = lax.optimization_barrier((gain, high_sends[0]))
    gain_sib = across(gain, 1)
    gain_far = across(gain, 2)
    gain_both = across(gain_far, 1)
    (gains,) = call(
        gain_kernel,
        [gain, gain_sib, gain_far, gain_both],
        [IN_VMEM] * 4,
        [held(1, depth, dtype=f32)],
    )

    normed = []
    for k in order:
        parts = [full[k]] if k < low else [near[k - low], across(near[k - low], 2)]
        normed += call(
            norm_kernel,
            [*parts, gains],
            [IN_VMEM] * (len(parts) + 1),
            [held(slots, depth)],
            flops=8 * slots * depth,
            moved=4 * slots * depth,
        )
    entering = [in_vmem(v) for v in normed + [across(v, 1) for v in normed]]
    blocks = hid // DEEP
    early, later = min(EARLY, blocks - 1), min(LATER, blocks - 1)
    weight = in_hbm(w_down[0])
    hidden, ahead = call(
        functools.partial(hidden_kernel, len(entering)),
        [*entering, in_vmem(w_gate[0]), in_vmem(w_up[0]), weight],
        [IN_VMEM] * (len(entering) + 2) + [IN_PLACE],
        [held(2 * rows, hid), held(early * DEEP, width)],
        scratch=[pltpu.SemaphoreType.DMA((early,))],
        flops=8 * rows * depth * hid,
        moved=2 * early * DEEP * width,
    )

    def down(first, ready, later):
        missing = blocks - ready.shape[0] // DEEP
        ahead = [held(later * DEEP, width)] if later else []
        sems = [pltpu.SemaphoreType.DMA((later,))] if later else []
        return call(
            functools.partial(down_kernel, first, later),
            [in_vmem(hidden), in_vmem(ready), weight],
            [IN_VMEM] * 2 + [IN_PLACE],
            [held(rows, width, dtype=f32), held(rows, width)] + ahead,
            scratch=[
                pltpu.VMEM((missing * DEEP, width), jnp.bfloat16),
                pltpu.VMEM((2 * rows, width), f32),
                pltpu.SemaphoreType.DMA((missing,)),
            ]
            + sems,
            mib=3 + missing * DEEP * width * 2 // 2**20 + 1,
            flops=2 * rows * depth * hid,
            moved=2 * (missing + later) * DEEP * width,
        )

    own_far, sib_far, kept = down(0, ahead, later)
    arrived_far = across(sib_far, 1)
    own_near, sib_near = down(blocks, kept, 0)
    arrived_near = across(sib_near, 1)
    crossing = call(
        merge_kernel,
        [own_far, arrived_far],
        [IN_VMEM] * 2,
        [held(slots, width)] * rounds,
        flops=rows * width,
        moved=8 * rows * width,
    )
    backs = []
    for k in reversed(order):
        (summed,) = call(
            functools.partial(fold_kernel, k),
            [own_near, arrived_near, across(crossing[k], 2)],
            [IN_VMEM] * 3,
            [held(slots, width)],
            flops=slots * width,
            moved=8 * slots * width,
        )
        backs.insert(0, between(summed, k))
    mine, send = call(
        functools.partial(combine_kernel, rounds),
        [weighted, moe_input, *backs],
        [IN_VMEM] * (2 + rounds),
        [held(tokens, feat, dtype=f32)] * 2,
        scratch=[pltpu.VMEM((tokens, width), f32)],
        mib=4,
        flops=2 * rows * tokens * width,
        moved=4 * rows * width,
    )
    return (mine + across(send, 1)).astype(jnp.bfloat16)


def gathered_layer(
    moe_input, norm_gain, expert_ids, combine_weights, capacity, w_gate, w_up, w_down
):
    tok_rows, feat_width = moe_input.shape
    experts = capacity.shape[0]
    depth = feat_width * lax.axis_size("mp")
    experts_total = lax.axis_size("expert")
    split_count = experts_total // experts
    slot_count = tok_rows // 2
    residual = moe_input.astype(jnp.float32)
    square_sum = lax.psum(jnp.sum(residual * residual, axis=1), "mp")
    normed = (
        residual * lax.rsqrt(square_sum / depth + 1e-05)[:, None] * norm_gain[None, :]
    ).astype(jnp.bfloat16)
    flat_ids = expert_ids.reshape(-1)
    one_hot = (flat_ids[:, None] == jnp.arange(experts)[None, :]).astype(jnp.int32)
    earlier = jnp.cumsum(one_hot, axis=0) - one_hot
    slot_rank = jnp.sum(earlier * one_hot, axis=1)
    limits = jnp.sum(one_hot * capacity[None, :], axis=1)
    kept_mask = slot_rank < limits
    slot_id = flat_ids * slot_count + slot_rank
    select = (jnp.arange(experts * slot_count)[:, None] == slot_id[None, :]) & kept_mask[None, :]
    chosen = select.reshape(experts * slot_count, tok_rows, TOP).sum(axis=-1).astype(jnp.bfloat16)
    packed = jnp.dot(chosen, normed, preferred_element_type=jnp.float32).astype(jnp.bfloat16)
    packed_view = packed.reshape(experts, 1, slot_count, feat_width)
    outgoing = jnp.broadcast_to(
        packed_view, (experts, split_count, slot_count, feat_width)
    ).reshape(experts_total, slot_count, feat_width)
    arrived = lax.all_to_all(outgoing, "expert", split_axis=0, concat_axis=0, tiled=True)
    slot_rows = arrived.reshape(experts_total * slot_count, feat_width)
    piece = lax.all_gather(slot_rows, "mp", axis=1, tiled=True)
    gate_sum = jnp.dot(piece, w_gate[0], preferred_element_type=jnp.float32)
    up_sum = jnp.dot(piece, w_up[0], preferred_element_type=jnp.float32)
    hidden = (jax.nn.silu(gate_sum) * up_sum).astype(jnp.bfloat16)
    down_terms = jnp.dot(hidden, w_down[0], preferred_element_type=jnp.float32)
    result = lax.psum_scatter(
        down_terms.astype(jnp.bfloat16), "mp", scatter_dimension=1, tiled=True
    )
    result = result.reshape(experts_total, slot_count, feat_width)
    returned = lax.all_to_all(result, "expert", split_axis=0, concat_axis=0, tiled=True)
    gathered = (
        returned.astype(jnp.float32)
        .reshape(experts, split_count, slot_count, feat_width)
        .sum(axis=1)
    )
    weighted = select.astype(jnp.float32) * combine_weights.reshape(-1)[None, :]
    weighted = weighted.reshape(experts * slot_count, tok_rows, TOP).sum(axis=-1)
    added = jnp.dot(
        weighted.T,
        gathered.reshape(experts * slot_count, feat_width),
        precision=lax.Precision.HIGHEST,
        preferred_element_type=jnp.float32,
    )
    return (residual + added).astype(jnp.bfloat16)


def attend_held(queries, k_cache, v_cache, lengths):
    seqs, heads, size = queries.shape
    tall = -(-heads // 16) * 16
    flat = queries.transpose(1, 0, 2).reshape(heads * seqs, size)
    positions = k_cache.shape[2]
    (out,) = call(
        functools.partial(attend_kernel, size ** (-0.5), seqs),
        [in_hbm(v) for v in (lengths, flat, k_cache, v_cache)],
        [IN_PLACE] * 4,
        [held(heads * seqs, size)],
        scratch=[
            pltpu.SMEM(lengths.shape, jnp.int32),
            pltpu.VMEM(flat.shape, flat.dtype),
            pltpu.VMEM(k_cache.shape, k_cache.dtype),
            pltpu.VMEM(v_cache.shape, v_cache.dtype),
            pltpu.VMEM((tall * seqs, size), jnp.float32),
            pltpu.VMEM((tall * seqs, positions), jnp.float32),
            pltpu.VMEM((tall * seqs, positions), jnp.bfloat16),
            pltpu.SemaphoreType.DMA((4,)),
        ],
        mib=7,
        flops=8 * seqs * tall * size * positions,
        moved=2 * k_cache.size * 2,
    )
    return out.reshape(heads, seqs, size).transpose(1, 0, 2)


def on_device(queries, k_cache, v_cache, lengths, moe_input, *rest):
    arriving = lax.axis_size("expert") * (moe_input.shape[0] // 2)
    paired = lax.axis_size("mp") == 4 and lax.axis_size("expert") % 4 == 0
    if paired and arriving <= VMEM_ROWS:
        context = attend_held(queries, k_cache, v_cache, lengths)
        return context, expert_layer(moe_input, *rest)
    context = attention(queries, k_cache, v_cache, lengths)
    return context, gathered_layer(moe_input, *rest)


def solution(mesh):
    in_specs = (
        P("expert", "mp", None),
        P("expert", "mp", None, None),
        P("expert", "mp", None, None),
        P("expert"),
        P("expert", "mp"),
        P("mp"),
        P("expert", None),
        P("expert", None),
        P(),
        P("expert", None, "mp"),
        P("expert", None, "mp"),
        P("expert", "mp", None),
    )
    out_specs = (P("expert", "mp", None), P("expert", "mp"))
    return jax.shard_map(
        on_device, mesh=mesh, in_specs=in_specs, out_specs=out_specs, check_vma=False
    )
```

profile of v0, /device:TPU:0, one launch (start us, length us, event | category | flops | bytes accessed | tf_op | source)
XLA Modules:
  0.0 70.0 jit_solution(7739454329600496479)
XLA Ops:
  1.2 2.6 %collective-permute-start.1 = (bf16[32,1536]{1,0:T(8,128)(2,1)}, bf16[32,1536]{1,0:T(8,128)(2,1)S(1)}, u32[]{:S(2)}, u32[]{:S(2)}) collective-permute-start(bf16[32,1536]{1,0:T(8,128)(2,1)} %residual.1), channel_id=1, source_target_pairs={{0,2},{1,3},{2,0},{3,1},{4,6},{5,7},{6,4},{7,5},{8,10},{9,11},{10,... | collective-permute-start | bytes 294920 | tf_op jit(solution)/shard_map/ppermute | solution.py:321
  3.7 1.0 %shard_map.132 = (bf16[64,32]{1,0:T(8,128)(2,1)S(1)}, f32[64,32]{1,0:T(8,128)S(1)}) custom-call(s32[2,32]{1,0:T(2,128)} %bitcast.22, f32[2,32]{1,0:T(2,128)} %bitcast.23, s32[8]{0:T(128)} %cap_at.1), custom_call_target="tpu_custom_call" | custom-call | flops 20000000000 | bytes 100000 | tf_op jit(solution)/shard_map/pallas_call | solution.py:292
  4.8 2.6 %collective-permute-done.1.refs_2_ = bf16[32,1536]{1,0:T(8,128)(2,1)S(1)} collective-permute-done((bf16[32,1536]{1,0:T(8,128)(2,1)}, bf16[32,1536]{1,0:T(8,128)(2,1)S(1)}, u32[]{:S(2)}, u32[]{:S(2)}) %collective-permute-start.1) | collective-permute-done | bytes 98336 | tf_op jit(solution)/shard_map/ppermute | solution.py:321
  7.5 2.9 %collective-permute-start.8 = (bf16[16,3072]{1,0:T(8,128)(2,1)S(1)}, bf16[16,3072]{1,0:T(8,128)(2,1)S(1)}, u32[]{:S(2)}, u32[]{:S(2)}) collective-permute-start(bf16[16,3072]{1,0:T(8,128)(2,1)S(1)} %get-tuple-element.31), channel_id=1, source_target_pairs={{0,16},{1,21},{2,18},{3,23},{4,20},{5,17},{6,22},{7,19},{8,24},{9,... | collective-permute-start | bytes 294920 | tf_op jit(solution)/shard_map/ppermute | solution.py:329
  10.5 1.4 %collective-permute-start.10 = (bf16[16,3072]{1,0:T(8,128)(2,1)S(1)}, bf16[16,3072]{1,0:T(8,128)(2,1)S(1)}, u32[]{:S(2)}, u32[]{:S(2)}) collective-permute-start(bf16[16,3072]{1,0:T(8,128)(2,1)S(1)} %get-tuple-element.34), channel_id=1, source_target_pairs={{0,24},{1,29},{2,26},{3,31},{4,28},{5,25},{6,30},{7,27},{8,16},{9,... | collective-permute-start | bytes 294920 | tf_op jit(solution)/shard_map/ppermute | solution.py:329
  12.5 0.8 %collective-permute-start.3 = (bf16[16,6144]{1,0:T(8,128)(2,1)S(1)}, bf16[16,6144]{1,0:T(8,128)(2,1)S(1)}, u32[]{:S(2)}, u32[]{:S(2)}) collective-permute-start(bf16[16,6144]{1,0:T(8,128)(2,1)S(1)} %get-tuple-element.29), channel_id=1, source_target_pairs={{0,0},{1,5},{2,2},{3,7},{4,4},{5,1},{6,6},{7,3},{8,8},{9,13},{10,1... | collective-permute-start | bytes 589832 | tf_op jit(solution)/shard_map/ppermute | solution.py:329
  13.4 6.2 %collective-permute-start.9 = (bf16[16,3072]{1,0:T(8,128)(2,1)S(1)}, bf16[16,3072]{1,0:T(8,128)(2,1)S(1)}, u32[]{:S(2)}, u32[]{:S(2)}) collective-permute-start(bf16[16,3072]{1,0:T(8,128)(2,1)S(1)} %collective-permute-done.8.refs_0_), channel_id=1, source_target_pairs={{0,2},{1,3},{2,0},{3,1},{4,6},{5,7},{6,4},{7,5},{8,10},{9,11},{10,... | collective-permute-start | bytes 294920 | tf_op jit(solution)/shard_map/ppermute | solution.py:321
  19.7 2.0 %collective-permute-start.5 = (f32[1,1536]{1,0:T(1,128)S(1)}, f32[1,1536]{1,0:T(1,128)S(1)}, u32[]{:S(2)}, u32[]{:S(2)}) collective-permute-start(f32[1,1536]{1,0:T(1,128)S(1)} %broadcast_in_dim.3.own), channel_id=1, source_target_pairs={{0,2},{1,3},{2,0},{3,1},{4,6},{5,7},{6,4},{7,5},{8,10},{9,11},{10,... | collective-permute-start | bytes 18440 | tf_op jit(solution)/shard_map/ppermute | solution.py:321
  21.7 2.8 %collective-permute-done.5.across = f32[1,1536]{1,0:T(1,128)S(1)} collective-permute-done((f32[1,1536]{1,0:T(1,128)S(1)}, f32[1,1536]{1,0:T(1,128)S(1)}, u32[]{:S(2)}, u32[]{:S(2)}) %collective-permute-start.5) | collective-permute-done | bytes 6176 | tf_op jit(solution)/shard_map/ppermute | solution.py:321
  24.5 1.2 %collective-permute-done.4.sibling = f32[1,1536]{1,0:T(1,128)S(1)} collective-permute-done((f32[1,1536]{1,0:T(1,128)S(1)}, f32[1,1536]{1,0:T(1,128)S(1)}, u32[]{:S(2)}, u32[]{:S(2)}) %collective-permute-start.4) | collective-permute-done | bytes 6176 | tf_op jit(solution)/shard_map/ppermute | solution.py:321
  25.8 1.0 %collective-permute-done.6.both = f32[1,1536]{1,0:T(1,128)S(1)} collective-permute-done((f32[1,1536]{1,0:T(1,128)S(1)}, f32[1,1536]{1,0:T(1,128)S(1)}, u32[]{:S(2)}, u32[]{:S(2)}) %collective-permute-start.6) | collective-permute-done | bytes 6176 | tf_op jit(solution)/shard_map/ppermute | solution.py:321
  30.1 7.5 %shard_map.140 = (bf16[128,2048]{1,0:T(8,128)(2,1)S(1)}, bf16[1536,3072]{1,0:T(8,128)(2,1)S(1)}) custom-call(bf16[16,6144]{1,0:T(8,128)(2,1)S(1)} %shard_map.136.refs_0_, bf16[16,6144]{1,0:T(8,128)(2,1)S(1)} %shard_map.137.refs_1_, bf16[16,6144]{1,0:T(8,128)(2,1)S(1)} %shard_map.138.refs_2_, bf16[16,6144]{1,0:T(8,128)(2,1)S(1)} %shard_map.139.refs_3_, ...), custom_call_target="tpu_custom_call" | custom-call | flops 6442450944 | bytes 9437184 | tf_op jit(solution)/shard_map/pallas_call | solution.py:292
  37.6 3.4 %shard_map.141 = (f32[64,3072]{1,0:T(8,128)S(1)}, bf16[64,3072]{1,0:T(8,128)(2,1)S(1)}, bf16[768,3072]{1,0:T(8,128)(2,1)S(1)}) custom-call(bf16[128,2048]{1,0:T(8,128)(2,1)S(1)} %get-tuple-element.35.hidden, bf16[1536,3072]{1,0:T(8,128)(2,1)S(1)} %get-tuple-element.36.ready, bf16[2048,6144]{1,0:T(8,128)(2,1)} %bitcast.19), custom_call_target="tpu_custom_call" | custom-call | flops 1610612736 | bytes 7864320 | tf_op jit(solution)/shard_map/pallas_call | solution.py:292
  41.4 3.7 %shard_map.142 = (f32[64,3072]{1,0:T(8,128)S(1)}, bf16[64,3072]{1,0:T(8,128)(2,1)S(1)}) custom-call(bf16[128,2048]{1,0:T(8,128)(2,1)S(1)} %get-tuple-element.35.hidden, bf16[768,3072]{1,0:T(8,128)(2,1)S(1)} %get-tuple-element.37.ready, bf16[2048,6144]{1,0:T(8,128)(2,1)} %bitcast.20), custom_call_target="tpu_custom_call" | custom-call | flops 1610612736 | bytes 7864320 | tf_op jit(solution)/shard_map/pallas_call | solution.py:292
  45.5 2.0 %collective-permute-start.24 = (bf16[16,3072]{1,0:T(8,128)(2,1)S(1)}, bf16[16,3072]{1,0:T(8,128)(2,1)S(1)}, u32[]{:S(2)}, u32[]{:S(2)}) collective-permute-start(bf16[16,3072]{1,0:T(8,128)(2,1)S(1)} %get-tuple-element.45), channel_id=1, source_target_pairs={{0,2},{1,3},{2,0},{3,1},{4,6},{5,7},{6,4},{7,5},{8,10},{9,11},{10,... | collective-permute-start | bytes 294920 | tf_op jit(solution)/shard_map/ppermute | solution.py:321
  47.6 1.9 %collective-permute-start.20 = (bf16[16,3072]{1,0:T(8,128)(2,1)S(1)}, bf16[16,3072]{1,0:T(8,128)(2,1)S(1)}, u32[]{:S(2)}, u32[]{:S(2)}) collective-permute-start(bf16[16,3072]{1,0:T(8,128)(2,1)S(1)} %get-tuple-element.43), channel_id=1, source_target_pairs={{0,2},{1,3},{2,0},{3,1},{4,6},{5,7},{6,4},{7,5},{8,10},{9,11},{10,... | collective-permute-start | bytes 294920 | tf_op jit(solution)/shard_map/ppermute | solution.py:321
  49.6 1.6 %collective-permute-done.24.crossed = bf16[16,3072]{1,0:T(8,128)(2,1)S(1)} collective-permute-done((bf16[16,3072]{1,0:T(8,128)(2,1)S(1)}, bf16[16,3072]{1,0:T(8,128)(2,1)S(1)}, u32[]{:S(2)}, u32[]{:S(2)}) %collective-permute-start.24) | collective-permute-done | bytes 98336 | tf_op jit(solution)/shard_map/ppermute | solution.py:321
  51.2 4.9 %collective-permute-start.25 = (bf16[16,3072]{1,0:T(8,128)(2,1)S(1)}, bf16[16,3072]{1,0:T(8,128)(2,1)S(1)}, u32[]{:S(2)}, u32[]{:S(2)}) collective-permute-start(bf16[16,3072]{1,0:T(8,128)(2,1)S(1)} %shard_map.147), channel_id=1, source_target_pairs={{0,24},{1,29},{2,26},{3,31},{4,28},{5,25},{6,30},{7,27},{8,16},{9,... | collective-permute-start | bytes 294920 | tf_op jit(solution)/shard_map/ppermute | solution.py:329
  56.2 1.3 %collective-permute-start.23 = (bf16[16,3072]{1,0:T(8,128)(2,1)S(1)}, bf16[16,3072]{1,0:T(8,128)(2,1)S(1)}, u32[]{:S(2)}, u32[]{:S(2)}) collective-permute-start(bf16[16,3072]{1,0:T(8,128)(2,1)S(1)} %shard_map.146), channel_id=1, source_target_pairs={{0,16},{1,21},{2,18},{3,23},{4,20},{5,17},{6,22},{7,19},{8,24},{9,... | collective-permute-start | bytes 294920 | tf_op jit(solution)/shard_map/ppermute | solution.py:329
  57.5 1.4 %collective-permute-start.21 = (bf16[16,3072]{1,0:T(8,128)(2,1)S(1)}, bf16[16,3072]{1,0:T(8,128)(2,1)S(1)}, u32[]{:S(2)}, u32[]{:S(2)}) collective-permute-start(bf16[16,3072]{1,0:T(8,128)(2,1)S(1)} %shard_map.145), channel_id=1, source_target_pairs={{0,8},{1,13},{2,10},{3,15},{4,12},{5,9},{6,14},{7,11},{8,0},{9,5},... | collective-permute-start | bytes 294920 | tf_op jit(solution)/shard_map/ppermute | solution.py:329
  58.9 0.7 collective-permute-start.19
  59.8 4.5 %collective-permute-done.23.refs_2_ = bf16[16,3072]{1,0:T(8,128)(2,1)S(1)} collective-permute-done((bf16[16,3072]{1,0:T(8,128)(2,1)S(1)}, bf16[16,3072]{1,0:T(8,128)(2,1)S(1)}, u32[]{:S(2)}, u32[]{:S(2)}) %collective-permute-start.23) | collective-permute-done | bytes 98336 | tf_op jit(solution)/shard_map/ppermute | solution.py:329
  65.0 3.8 %shard_map.131 = bf16[384,128]{1,0:T(8,128)(2,1)S(1)} custom-call(s32[32]{0:T(128)} %lengths_at.1, bf16[384,128]{1,0:T(8,128)(2,1)} %bitcast.21, bf16[32,2,128,128]{3,2,1,0:T(8,128)(2,1)} %k_at.1, bf16[32,2,128,128]{3,2,1,0:T(8,128)(2,1)} %v_at.1), custom_call_target="tpu_custom_call" | custom-call | flops 67108864 | bytes 4194304 | tf_op jit(solution)/shard_map/pallas_call | solution.py:292
  69.4 0.7 add_convert_fusion
  (81 shorter events, 7.3 us)
Async XLA Ops:
  0.6 4.1 %collective-permute-start = (bf16[32,1536]{1,0:T(8,128)(2,1)}, bf16[32,1536]{1,0:T(8,128)(2,1)S(1)}, u32[]{:S(2)}, u32[]{:S(2)}) collective-permute-start(bf16[32,1536]{1,0:T(8,128)(2,1)} %residual.1), channel_id=1, source_target_pairs={{0,1},{1,0},{2,3},{3,2},{4,5},{5,4},{6,7},{7,6},{8,9},{9,8},{10,11... | collective-permute-start | bytes 294920 | tf_op jit(solution)/shard_map/ppermute | solution.py:321
  1.2 6.2 %collective-permute-start.1 = (bf16[32,1536]{1,0:T(8,128)(2,1)}, bf16[32,1536]{1,0:T(8,128)(2,1)S(1)}, u32[]{:S(2)}, u32[]{:S(2)}) collective-permute-start(bf16[32,1536]{1,0:T(8,128)(2,1)} %residual.1), channel_id=1, source_target_pairs={{0,2},{1,3},{2,0},{3,1},{4,6},{5,7},{6,4},{7,5},{8,10},{9,11},{10,... | collective-permute-start | bytes 294920 | tf_op jit(solution)/shard_map/ppermute | solution.py:321
  7.3 4.6 %collective-permute-start.2 = (bf16[32,1536]{1,0:T(8,128)(2,1)S(1)}, bf16[32,1536]{1,0:T(8,128)(2,1)S(1)}, u32[]{:S(2)}, u32[]{:S(2)}) collective-permute-start(bf16[32,1536]{1,0:T(8,128)(2,1)S(1)} %collective-permute-done.1.refs_2_), channel_id=1, source_target_pairs={{0,1},{1,0},{2,3},{3,2},{4,5},{5,4},{6,7},{7,6},{8,9},{9,8},{10,11... | collective-permute-start | bytes 294920 | tf_op jit(solution)/shard_map/ppermute | solution.py:321
  7.5 5.9 %collective-permute-start.8 = (bf16[16,3072]{1,0:T(8,128)(2,1)S(1)}, bf16[16,3072]{1,0:T(8,128)(2,1)S(1)}, u32[]{:S(2)}, u32[]{:S(2)}) collective-permute-start(bf16[16,3072]{1,0:T(8,128)(2,1)S(1)} %get-tuple-element.31), channel_id=1, source_target_pairs={{0,16},{1,21},{2,18},{3,23},{4,20},{5,17},{6,22},{7,19},{8,24},{9,... | collective-permute-start | bytes 294920 | tf_op jit(solution)/shard_map/ppermute | solution.py:329
  10.5 9.1 %collective-permute-start.10 = (bf16[16,3072]{1,0:T(8,128)(2,1)S(1)}, bf16[16,3072]{1,0:T(8,128)(2,1)S(1)}, u32[]{:S(2)}, u32[]{:S(2)}) collective-permute-start(bf16[16,3072]{1,0:T(8,128)(2,1)S(1)} %get-tuple-element.34), channel_id=1, source_target_pairs={{0,24},{1,29},{2,26},{3,31},{4,28},{5,25},{6,30},{7,27},{8,16},{9,... | collective-permute-start | bytes 294920 | tf_op jit(solution)/shard_map/ppermute | solution.py:329
  12.2 15.7 %collective-permute-start.7 = (bf16[16,6144]{1,0:T(8,128)(2,1)S(1)}, bf16[16,6144]{1,0:T(8,128)(2,1)S(1)}, u32[]{:S(2)}, u32[]{:S(2)}) collective-permute-start(bf16[16,6144]{1,0:T(8,128)(2,1)S(1)} %get-tuple-element.33), channel_id=1, source_target_pairs={{0,8},{1,13},{2,10},{3,15},{4,12},{5,9},{6,14},{7,11},{8,0},{9,5},... | collective-permute-start | bytes 589832 | tf_op jit(solution)/shard_map/ppermute | solution.py:329
  12.5 15.8 %collective-permute-start.3 = (bf16[16,6144]{1,0:T(8,128)(2,1)S(1)}, bf16[16,6144]{1,0:T(8,128)(2,1)S(1)}, u32[]{:S(2)}, u32[]{:S(2)}) collective-permute-start(bf16[16,6144]{1,0:T(8,128)(2,1)S(1)} %get-tuple-element.29), channel_id=1, source_target_pairs={{0,0},{1,5},{2,2},{3,7},{4,4},{5,1},{6,6},{7,3},{8,8},{9,13},{10,1... | collective-permute-start | bytes 589832 | tf_op jit(solution)/shard_map/ppermute | solution.py:329
  13.4 13.4 %collective-permute-start.9 = (bf16[16,3072]{1,0:T(8,128)(2,1)S(1)}, bf16[16,3072]{1,0:T(8,128)(2,1)S(1)}, u32[]{:S(2)}, u32[]{:S(2)}) collective-permute-start(bf16[16,3072]{1,0:T(8,128)(2,1)S(1)} %collective-permute-done.8.refs_0_), channel_id=1, source_target_pairs={{0,2},{1,3},{2,0},{3,1},{4,6},{5,7},{6,4},{7,5},{8,10},{9,11},{10,... | collective-permute-start | bytes 294920 | tf_op jit(solution)/shard_map/ppermute | solution.py:321
  19.7 7.6 %collective-permute-start.11 = (bf16[16,3072]{1,0:T(8,128)(2,1)S(1)}, bf16[16,3072]{1,0:T(8,128)(2,1)S(1)}, u32[]{:S(2)}, u32[]{:S(2)}) collective-permute-start(bf16[16,3072]{1,0:T(8,128)(2,1)S(1)} %collective-permute-done.10.refs_0_), channel_id=1, source_target_pairs={{0,2},{1,3},{2,0},{3,1},{4,6},{5,7},{6,4},{7,5},{8,10},{9,11},{10,... | collective-permute-start | bytes 294920 | tf_op jit(solution)/shard_map/ppermute | solution.py:321
  19.7 4.8 %collective-permute-start.5 = (f32[1,1536]{1,0:T(1,128)S(1)}, f32[1,1536]{1,0:T(1,128)S(1)}, u32[]{:S(2)}, u32[]{:S(2)}) collective-permute-start(f32[1,1536]{1,0:T(1,128)S(1)} %broadcast_in_dim.3.own), channel_id=1, source_target_pairs={{0,2},{1,3},{2,0},{3,1},{4,6},{5,7},{6,4},{7,5},{8,10},{9,11},{10,... | collective-permute-start | bytes 18440 | tf_op jit(solution)/shard_map/ppermute | solution.py:321
  27.0 1.9 %collective-permute-start.14 = (bf16[16,6144]{1,0:T(8,128)(2,1)S(1)}, bf16[16,6144]{1,0:T(8,128)(2,1)S(1)}, u32[]{:S(2)}, u32[]{:S(2)}) collective-permute-start(bf16[16,6144]{1,0:T(8,128)(2,1)S(1)} %shard_map.138.refs_2_), channel_id=1, source_target_pairs={{0,1},{1,0},{2,3},{3,2},{4,5},{5,4},{6,7},{7,6},{8,9},{9,8},{10,11... | collective-permute-start | bytes 589832 | tf_op jit(solution)/shard_map/ppermute | solution.py:321
  27.5 1.5 %collective-permute-start.15 = (bf16[16,6144]{1,0:T(8,128)(2,1)S(1)}, bf16[16,6144]{1,0:T(8,128)(2,1)S(1)}, u32[]{:S(2)}, u32[]{:S(2)}) collective-permute-start(bf16[16,6144]{1,0:T(8,128)(2,1)S(1)} %shard_map.139.refs_3_), channel_id=1, source_target_pairs={{0,1},{1,0},{2,3},{3,2},{4,5},{5,4},{6,7},{7,6},{8,9},{9,8},{10,11... | collective-permute-start | bytes 589832 | tf_op jit(solution)/shard_map/ppermute | solution.py:321
  28.1 1.5 %collective-permute-start.13 = (bf16[16,6144]{1,0:T(8,128)(2,1)S(1)}, bf16[16,6144]{1,0:T(8,128)(2,1)S(1)}, u32[]{:S(2)}, u32[]{:S(2)}) collective-permute-start(bf16[16,6144]{1,0:T(8,128)(2,1)S(1)} %shard_map.137.refs_1_), channel_id=1, source_target_pairs={{0,1},{1,0},{2,3},{3,2},{4,5},{5,4},{6,7},{7,6},{8,9},{9,8},{10,11... | collective-permute-start | bytes 589832 | tf_op jit(solution)/shard_map/ppermute | solution.py:321
  41.0 4.4 %collective-permute-start.17 = (bf16[64,3072]{1,0:T(8,128)(2,1)S(1)}, bf16[64,3072]{1,0:T(8,128)(2,1)S(1)}, u32[]{:S(2)}, u32[]{:S(2)}) collective-permute-start(bf16[64,3072]{1,0:T(8,128)(2,1)S(1)} %get-tuple-element.41), channel_id=1, source_target_pairs={{0,1},{1,0},{2,3},{3,2},{4,5},{5,4},{6,7},{7,6},{8,9},{9,8},{10,11... | collective-permute-start | bytes 1179656 | tf_op jit(solution)/shard_map/ppermute | solution.py:321
  45.1 4.5 %collective-permute-start.16 = (bf16[64,3072]{1,0:T(8,128)(2,1)S(1)}, bf16[64,3072]{1,0:T(8,128)(2,1)S(1)}, u32[]{:S(2)}, u32[]{:S(2)}) collective-permute-start(bf16[64,3072]{1,0:T(8,128)(2,1)S(1)} %get-tuple-element.39), channel_id=1, source_target_pairs={{0,1},{1,0},{2,3},{3,2},{4,5},{5,4},{6,7},{7,6},{8,9},{9,8},{10,11... | collective-permute-start | bytes 1179656 | tf_op jit(solution)/shard_map/ppermute | solution.py:321
  45.5 5.7 %collective-permute-start.24 = (bf16[16,3072]{1,0:T(8,128)(2,1)S(1)}, bf16[16,3072]{1,0:T(8,128)(2,1)S(1)}, u32[]{:S(2)}, u32[]{:S(2)}) collective-permute-start(bf16[16,3072]{1,0:T(8,128)(2,1)S(1)} %get-tuple-element.45), channel_id=1, source_target_pairs={{0,2},{1,3},{2,0},{3,1},{4,6},{5,7},{6,4},{7,5},{8,10},{9,11},{10,... | collective-permute-start | bytes 294920 | tf_op jit(solution)/shard_map/ppermute | solution.py:321
  47.5 8.6 %collective-permute-start.22 = (bf16[16,3072]{1,0:T(8,128)(2,1)S(1)}, bf16[16,3072]{1,0:T(8,128)(2,1)S(1)}, u32[]{:S(2)}, u32[]{:S(2)}) collective-permute-start(bf16[16,3072]{1,0:T(8,128)(2,1)S(1)} %get-tuple-element.44), channel_id=1, source_target_pairs={{0,2},{1,3},{2,0},{3,1},{4,6},{5,7},{6,4},{7,5},{8,10},{9,11},{10,... | collective-permute-start | bytes 294920 | tf_op jit(solution)/shard_map/ppermute | solution.py:321
  47.6 9.9 %collective-permute-start.20 = (bf16[16,3072]{1,0:T(8,128)(2,1)S(1)}, bf16[16,3072]{1,0:T(8,128)(2,1)S(1)}, u32[]{:S(2)}, u32[]{:S(2)}) collective-permute-start(bf16[16,3072]{1,0:T(8,128)(2,1)S(1)} %get-tuple-element.43), channel_id=1, source_target_pairs={{0,2},{1,3},{2,0},{3,1},{4,6},{5,7},{6,4},{7,5},{8,10},{9,11},{10,... | collective-permute-start | bytes 294920 | tf_op jit(solution)/shard_map/ppermute | solution.py:321
  49.5 9.4 %collective-permute-start.18 = (bf16[16,3072]{1,0:T(8,128)(2,1)S(1)}, bf16[16,3072]{1,0:T(8,128)(2,1)S(1)}, u32[]{:S(2)}, u32[]{:S(2)}) collective-permute-start(bf16[16,3072]{1,0:T(8,128)(2,1)S(1)} %get-tuple-element.42), channel_id=1, source_target_pairs={{0,2},{1,3},{2,0},{3,1},{4,6},{5,7},{6,4},{7,5},{8,10},{9,11},{10,... | collective-permute-start | bytes 294920 | tf_op jit(solution)/shard_map/ppermute | solution.py:321
  51.2 8.5 %collective-permute-start.25 = (bf16[16,3072]{1,0:T(8,128)(2,1)S(1)}, bf16[16,3072]{1,0:T(8,128)(2,1)S(1)}, u32[]{:S(2)}, u32[]{:S(2)}) collective-permute-start(bf16[16,3072]{1,0:T(8,128)(2,1)S(1)} %shard_map.147), channel_id=1, source_target_pairs={{0,24},{1,29},{2,26},{3,31},{4,28},{5,25},{6,30},{7,27},{8,16},{9,... | collective-permute-start | bytes 294920 | tf_op jit(solution)/shard_map/ppermute | solution.py:329
  56.2 8.1 %collective-permute-start.23 = (bf16[16,3072]{1,0:T(8,128)(2,1)S(1)}, bf16[16,3072]{1,0:T(8,128)(2,1)S(1)}, u32[]{:S(2)}, u32[]{:S(2)}) collective-permute-start(bf16[16,3072]{1,0:T(8,128)(2,1)S(1)} %shard_map.146), channel_id=1, source_target_pairs={{0,16},{1,21},{2,18},{3,23},{4,20},{5,17},{6,22},{7,19},{8,24},{9,... | collective-permute-start | bytes 294920 | tf_op jit(solution)/shard_map/ppermute | solution.py:329
  57.5 6.8 %collective-permute-start.21 = (bf16[16,3072]{1,0:T(8,128)(2,1)S(1)}, bf16[16,3072]{1,0:T(8,128)(2,1)S(1)}, u32[]{:S(2)}, u32[]{:S(2)}) collective-permute-start(bf16[16,3072]{1,0:T(8,128)(2,1)S(1)} %shard_map.145), channel_id=1, source_target_pairs={{0,8},{1,13},{2,10},{3,15},{4,12},{5,9},{6,14},{7,11},{8,0},{9,5},... | collective-permute-start | bytes 294920 | tf_op jit(solution)/shard_map/ppermute | solution.py:329
  58.9 5.3 %collective-permute-start.19 = (bf16[16,3072]{1,0:T(8,128)(2,1)S(1)}, bf16[16,3072]{1,0:T(8,128)(2,1)S(1)}, u32[]{:S(2)}, u32[]{:S(2)}) collective-permute-start(bf16[16,3072]{1,0:T(8,128)(2,1)S(1)} %shard_map.144), channel_id=1, source_target_pairs={{0,0},{1,5},{2,2},{3,7},{4,4},{5,1},{6,6},{7,3},{8,8},{9,13},{10,1... | collective-permute-start | bytes 294920 | tf_op jit(solution)/shard_map/ppermute | solution.py:329
  64.8 4.6 %collective-permute-start.26 = (f32[32,1536]{1,0:T(8,128)S(1)}, f32[32,1536]{1,0:T(8,128)S(1)}, u32[]{:S(2)}, u32[]{:S(2)}) collective-permute-start(f32[32,1536]{1,0:T(8,128)S(1)} %get-tuple-element.47), channel_id=1, source_target_pairs={{0,1},{1,0},{2,3},{3,2},{4,5},{5,4},{6,7},{7,6},{8,9},{9,8},{10,11... | collective-permute-start | bytes 589832 | tf_op jit(solution)/shard_map/ppermute | solution.py:321
  (17 other events, 243.2 us)
where the time goes:
time: 70.2 us; the launch traced here: 70 us
  starting transfers between devices  31.5 us (45%)
  Pallas kernels  21.2 us (30%)
  waiting for transfers between devices  15 us (21%)
  between operations  0.97 us (1%)
  local copies, waits for them, and re-layouts  0.71 us (1%)
    pallas_call x18, Pallas kernels, call(): pl.pallas_call(body, out_shape=outs, in_specs=specs, out_specs=[IN_VMEM]...  21.2 us
    ppermute x19, starting transfers between devices, across(): return lax.ppermute(v, 'mp', [(i, i ^ bit) for i in range(members)])  17.8 us
    ppermute x8, starting transfers between devices, between(): return lax.ppermute(v, ('expert', 'mp'), pairs)  13.7 us
    ppermute x19, waiting for transfers between devices, across(): return lax.ppermute(v, 'mp', [(i, i ^ bit) for i in range(members)])  10.3 us
    ppermute x8, waiting for transfers between devices, between(): return lax.ppermute(v, ('expert', 'mp'), pairs)  4.75 us
  transfers between devices with their start and end apart: 27, of which 11 were waited for; matrix products, arithmetic and copies ran while one was open for 1% of the time, Pallas kernels for 14%

commit v1 on v0

--- a/solution.py
+++ b/solution.py
@@ -11,7 +11,9 @@
 TOP = 2
 WIDE = 512
 DEEP = 256
-EARLY = 6
+RING = 8
+SPAN = 8
+EARLY = 7
 LATER = 3
 VMEM_ROWS = 128
 ROUTE_FLOPS = 2e10
@@ -40,55 +42,73 @@
     return context.astype(jnp.bfloat16).reshape(seq_count, head_count, head_size)
 
 
-def attend_kernel(scale, seqs, lengths_at, q_at, k_at, v_at, out, lengths, q, k, v, wide, score, prob, sems):
-    copies = [
+def attend_kernel(scale, seqs, lengths_at, q_at, k_at, v_at, out, lengths, q, ring, wide, score, prob, sems):
+    span = ring.shape[1]
+    parts = seqs // span
+    slots = ring.shape[0]
+    near = [
         pltpu.make_async_copy(source, target, sems.at[i])
-        for i, (source, target) in enumerate(
-            ((lengths_at, lengths), (q_at, q), (k_at, k), (v_at, v))
-        )
+        for i, (source, target) in enumerate(((lengths_at, lengths), (q_at, q)))
     ]
-    for copy in copies:
+
+    def load(i):
+        source = (k_at if i < parts else v_at).at[i % parts * span : (i % parts + 1) * span]
+        return pltpu.make_async_copy(source, ring.at[i % slots], sems.at[2 + i])
+
+    def turn(i):
+        if i + slots < 2 * parts:
+            load(i + slots).start()
+
+    for copy in near:
         copy.start()
+    for i in range(slots):
+        load(i).start()
     heads, size = q.shape[0] // seqs, q.shape[1]
-    kv = k.shape[1]
+    kv = ring.shape[2]
     tall = wide.shape[0] // seqs
     group = heads // kv
-    positions = k.shape[2]
+    positions = ring.shape[3]
     row = lax.broadcasted_iota(jnp.int32, (tall, positions), 0)
     lane = lax.broadcasted_iota(jnp.int32, (tall, positions), 1)
-    copies[0].wait()
-    copies[1].wait()
+    for copy in near:
+        copy.wait()
     wide[: heads * seqs, :] = q[...].astype(jnp.float32)
     wide[heads * seqs :, :] = jnp.zeros(((tall - heads) * seqs, size), jnp.float32)
-    copies[2].wait()
-    for b in range(seqs):
-        queries = wide[pl.ds(b, tall, stride=seqs), :].astype(jnp.bfloat16)
-        total = None
-        for j in range(kv):
-            dots = lax.dot_general(
-                queries,
-                k[b, j],
-                (((1,), (1,)), ((), ())),
-                preferred_element_type=jnp.float32,
-            )
-            total = dots if total is None else jnp.where(row < j * group, total, dots)
-        live = lane < lengths[b]
-        score[b * tall : (b + 1) * tall, :] = jnp.where(live, total * scale, -jnp.inf)
+    for i in range(parts):
+        load(i).wait()
+        for at in range(span):
+            b = i * span + at
+            queries = wide[pl.ds(b, tall, stride=seqs), :].astype(jnp.bfloat16)
+            total = None
+            for j in range(kv):
+                dots = lax.dot_general(
+                    queries,
+                    ring[i % slots, at, j],
+                    (((1,), (1,)), ((), ())),
+                    preferred_element_type=jnp.float32,
+                )
+                total = dots if total is None else jnp.where(row < j * group, total, dots)
+            live = lane < lengths[b]
+            score[b * tall : (b + 1) * tall, :] = jnp.where(live, total * scale, -jnp.inf)
+        turn(i)
     top = jnp.max(score[...], axis=-1, keepdims=True)
     expo = jnp.exp(score[...] - top)
     prob[...] = (expo / jnp.sum(expo, axis=-1, keepdims=True)).astype(jnp.bfloat16)
-    copies[3].wait()
-    for b in range(seqs):
-        probs = prob[b * tall : (b + 1) * tall, :].astype(jnp.float32)
-        total = jnp.zeros((tall, size), jnp.float32)
-        for j in range(kv):
-            mine = (row >= j * group) & (row < (j + 1) * group)
-            total = total + jnp.dot(
-                jnp.where(mine, probs, 0.0).astype(jnp.bfloat16),
-                v[b, j],
-                preferred_element_type=jnp.float32,
-            )
-        wide[pl.ds(b, tall, stride=seqs), :] = total
+    for i in range(parts, 2 * parts):
+        load(i).wait()
+        for at in range(span):
+            b = (i - parts) * span + at
+            probs = prob[b * tall : (b + 1) * tall, :].astype(jnp.float32)
+            total = jnp.zeros((tall, size), jnp.float32)
+            for j in range(kv):
+                mine = (row >= j * group) & (row < (j + 1) * group)
+                total = total + jnp.dot(
+                    jnp.where(mine, probs, 0.0).astype(jnp.bfloat16),
+                    ring[i % slots, at, j],
+                    preferred_element_type=jnp.float32,
+                )
+            wide[pl.ds(b, tall, stride=seqs), :] = total
+        turn(i)
     out[...] = wide[: heads * seqs, :].astype(jnp.bfloat16)
 
 
@@ -345,7 +365,9 @@
         flops=ROUTE_FLOPS,
         moved=1e5,
     )
-    gain, sibling, select = lax.optimization_barrier((norm_gain[None, :], sibling, select))
+    gain, select = lax.optimization_barrier((norm_gain, select))
+    gain = gain[None, :]
+    gain, sibling, select = lax.optimization_barrier((gain, sibling, select))
 
     def pack(first, count, total, sources):
         return call(
@@ -374,18 +396,22 @@
         [held(1, depth, dtype=f32)],
     )
 
-    normed = []
-    for k in order:
-        parts = [full[k]] if k < low else [near[k - low], across(near[k - low], 2)]
-        normed += call(
+    def norm(parts):
+        return call(
             norm_kernel,
             [*parts, gains],
             [IN_VMEM] * (len(parts) + 1),
             [held(slots, depth)],
             flops=8 * slots * depth,
             moved=4 * slots * depth,
-        )
-    entering = [in_vmem(v) for v in normed + [across(v, 1) for v in normed]]
+        )[0]
+
+    normed = [norm([part]) for part in full]
+    far = [across(part, 2) for part in near]
+    far[:-1], normed = lax.optimization_barrier((far[:-1], normed))
+    normed += [norm([here, there]) for here, there in zip(near, far)]
+    traded = [across(v, 1) for v in normed]
+    entering = [in_vmem(v) for v in normed + traded]
     blocks = hid // DEEP
     early, later = min(EARLY, blocks - 1), min(LATER, blocks - 1)
     weight = in_hbm(w_down[0])
@@ -524,12 +550,11 @@
         scratch=[
             pltpu.SMEM(lengths.shape, jnp.int32),
             pltpu.VMEM(flat.shape, flat.dtype),
-            pltpu.VMEM(k_cache.shape, k_cache.dtype),
-            pltpu.VMEM(v_cache.shape, v_cache.dtype),
+            pltpu.VMEM((RING, SPAN) + k_cache.shape[1:], k_cache.dtype),
             pltpu.VMEM((tall * seqs, size), jnp.float32),
             pltpu.VMEM((tall * seqs, positions), jnp.float32),
             pltpu.VMEM((tall * seqs, positions), jnp.bfloat16),
-            pltpu.SemaphoreType.DMA((4,)),
+            pltpu.SemaphoreType.DMA((2 + 2 * (seqs // SPAN),)),
         ],
         mib=7,
         flops=8 * seqs * tall * size * positions,

time: 70.2 us -> 70.1 us (level)
  waiting for transfers between devices: 15 us -> 22.3 us
  starting transfers between devices: 31.5 us -> 24.3 us
    ppermute x8, waiting for transfers between devices: 4.75 us -> 9.21 us  [between(): return lax.ppermute(v, ('expert', 'mp'), pairs)]
    ppermute x8, starting transfers between devices: 13.7 us -> 9.68 us  [between(): return lax.ppermute(v, ('expert', 'mp'), pairs)]
    ppermute x19, starting transfers between devices: 17.8 us -> 14.6 us  [across(): return lax.ppermute(v, 'mp', [(i, i ^ bit) for i in range(members)])]
    ppermute x19, waiting for transfers between devices: 10.3 us -> 13 us  [across(): return lax.ppermute(v, 'mp', [(i, i ^ bit) for i in range(members)])]
  transfers between devices with their start and end apart: 27 -> 27, of which waited for: 11 -> 15; matrix products, arithmetic and copies ran while one was open for 1% -> 1% of each run, Pallas kernels for 14% -> 14%
where the time goes in v1:
time: 70.1 us; the launch traced here: 69.9 us
  starting transfers between devices  24.3 us (35%)
  waiting for transfers between devices  22.3 us (32%)
  Pallas kernels  20.9 us (30%)
  between operations  1.03 us (1%)
  local copies, waits for them, and re-layouts  0.72 us (1%)
    pallas_call x18, Pallas kernels, call(): pl.pallas_call(body, out_shape=outs, in_specs=specs, out_specs=[IN_VMEM]...  20.9 us
    ppermute x19, starting transfers between devices, across(): return lax.ppermute(v, 'mp', [(i, i ^ bit) for i in range(members)])  14.6 us
    ppermute x19, waiting for transfers between devices, across(): return lax.ppermute(v, 'mp', [(i, i ^ bit) for i in range(members)])  13 us
    ppermute x8, starting transfers between devices, between(): return lax.ppermute(v, ('expert', 'mp'), pairs)  9.68 us
    ppermute x8, waiting for transfers between devices, between(): return lax.ppermute(v, ('expert', 'mp'), pairs)  9.21 us
  transfers between devices with their start and end apart: 27, of which 15 were waited for; matrix products, arithmetic and copies ran while one was open for 1% of the time, Pallas kernels for 14%

profile of v1, /device:TPU:0, one launch (start us, length us, event | category | flops | bytes accessed | tf_op | source)
XLA Modules:
  0.0 69.9 jit_solution(11971821263221580985)
XLA Ops:
  1.2 2.6 %collective-permute-start.3 = (bf16[32,1536]{1,0:T(8,128)(2,1)}, bf16[32,1536]{1,0:T(8,128)(2,1)S(1)}, u32[]{:S(2)}, u32[]{:S(2)}) collective-permute-start(bf16[32,1536]{1,0:T(8,128)(2,1)} %residual.1), channel_id=1, source_target_pairs={{0,2},{1,3},{2,0},{3,1},{4,6},{5,7},{6,4},{7,5},{8,10},{9,11},{10,... | collective-permute-start | bytes 294920 | tf_op jit(solution)/shard_map/ppermute | solution.py:341
  3.7 1.0 %shard_map.132 = (bf16[64,32]{1,0:T(8,128)(2,1)S(1)}, f32[64,32]{1,0:T(8,128)S(1)}) custom-call(s32[2,32]{1,0:T(2,128)} %bitcast.22, f32[2,32]{1,0:T(2,128)} %bitcast.23, s32[8]{0:T(128)} %cap_at.1), custom_call_target="tpu_custom_call" | custom-call | flops 20000000000 | bytes 100000 | tf_op jit(solution)/shard_map/pallas_call | solution.py:312
  4.8 2.6 %collective-permute-done.3.refs_2_ = bf16[32,1536]{1,0:T(8,128)(2,1)S(1)} collective-permute-done((bf16[32,1536]{1,0:T(8,128)(2,1)}, bf16[32,1536]{1,0:T(8,128)(2,1)S(1)}, u32[]{:S(2)}, u32[]{:S(2)}) %collective-permute-start.3) | collective-permute-done | bytes 98336 | tf_op jit(solution)/shard_map/ppermute | solution.py:341
  7.7 3.9 %collective-permute-start.10 = (bf16[16,3072]{1,0:T(8,128)(2,1)S(1)}, bf16[16,3072]{1,0:T(8,128)(2,1)S(1)}, u32[]{:S(2)}, u32[]{:S(2)}) collective-permute-start(bf16[16,3072]{1,0:T(8,128)(2,1)S(1)} %get-tuple-element.44), channel_id=1, source_target_pairs={{0,24},{1,29},{2,26},{3,31},{4,28},{5,25},{6,30},{7,27},{8,16},{9,... | collective-permute-start | bytes 294920 | tf_op jit(solution)/shard_map/ppermute | solution.py:349
  11.9 0.8 %collective-permute-start.5 = (bf16[16,6144]{1,0:T(8,128)(2,1)S(1)}, bf16[16,6144]{1,0:T(8,128)(2,1)S(1)}, u32[]{:S(2)}, u32[]{:S(2)}) collective-permute-start(bf16[16,6144]{1,0:T(8,128)(2,1)S(1)} %get-tuple-element.37), channel_id=1, source_target_pairs={{0,0},{1,5},{2,2},{3,7},{4,4},{5,1},{6,6},{7,3},{8,8},{9,13},{10,1... | collective-permute-start | bytes 589832 | tf_op jit(solution)/shard_map/ppermute | solution.py:349
  12.7 1.5 %collective-permute-start.1 = (bf16[16,3072]{1,0:T(8,128)(2,1)S(1)}, bf16[16,3072]{1,0:T(8,128)(2,1)S(1)}, u32[]{:S(2)}, u32[]{:S(2)}) collective-permute-start(bf16[16,3072]{1,0:T(8,128)(2,1)S(1)} %get-tuple-element.36), channel_id=1, source_target_pairs={{0,16},{1,21},{2,18},{3,23},{4,20},{5,17},{6,22},{7,19},{8,24},{9,... | collective-permute-start | bytes 294920 | tf_op jit(solution)/shard_map/ppermute | solution.py:349
  14.6 1.9 %collective-permute-start.11 = (bf16[16,3072]{1,0:T(8,128)(2,1)S(1)}, bf16[16,3072]{1,0:T(8,128)(2,1)S(1)}, u32[]{:S(2)}, u32[]{:S(2)}) collective-permute-start(bf16[16,3072]{1,0:T(8,128)(2,1)S(1)} %collective-permute-done.10.refs_0_), channel_id=1, source_target_pairs={{0,2},{1,3},{2,0},{3,1},{4,6},{5,7},{6,4},{7,5},{8,10},{9,11},{10,... | collective-permute-start | bytes 294920 | tf_op jit(solution)/shard_map/ppermute | solution.py:341
  16.5 4.1 %collective-permute-done.1.refs_0_ = bf16[16,3072]{1,0:T(8,128)(2,1)S(1)} collective-permute-done((bf16[16,3072]{1,0:T(8,128)(2,1)S(1)}, bf16[16,3072]{1,0:T(8,128)(2,1)S(1)}, u32[]{:S(2)}, u32[]{:S(2)}) %collective-permute-start.1) | collective-permute-done | bytes 98336 | tf_op jit(solution)/shard_map/ppermute | solution.py:349
  20.7 1.5 %collective-permute-start.2 = (bf16[16,3072]{1,0:T(8,128)(2,1)S(1)}, bf16[16,3072]{1,0:T(8,128)(2,1)S(1)}, u32[]{:S(2)}, u32[]{:S(2)}) collective-permute-start(bf16[16,3072]{1,0:T(8,128)(2,1)S(1)} %collective-permute-done.1.refs_0_), channel_id=1, source_target_pairs={{0,2},{1,3},{2,0},{3,1},{4,6},{5,7},{6,4},{7,5},{8,10},{9,11},{10,... | collective-permute-start | bytes 294920 | tf_op jit(solution)/shard_map/ppermute | solution.py:341
  22.7 3.1 %collective-permute-done.7.across = f32[1,1536]{1,0:T(1,128)S(1)} collective-permute-done((f32[1,1536]{1,0:T(1,128)S(1)}, f32[1,1536]{1,0:T(1,128)S(1)}, u32[]{:S(2)}, u32[]{:S(2)}) %collective-permute-start.7) | collective-permute-done | bytes 6176 | tf_op jit(solution)/shard_map/ppermute | solution.py:341
  25.8 1.2 %collective-permute-start.6 = (f32[1,1536]{1,0:T(1,128)S(1)}, f32[1,1536]{1,0:T(1,128)S(1)}, u32[]{:S(2)}, u32[]{:S(2)}) collective-permute-start(f32[1,1536]{1,0:T(1,128)S(1)} %broadcast_in_dim.3.own), channel_id=1, source_target_pairs={{0,1},{1,0},{2,3},{3,2},{4,5},{5,4},{6,7},{7,6},{8,9},{9,8},{10,11... | collective-permute-start | bytes 18440 | tf_op jit(solution)/shard_map/ppermute | solution.py:341
  26.9 0.8 %collective-permute-done.6.sibling = f32[1,1536]{1,0:T(1,128)S(1)} collective-permute-done((f32[1,1536]{1,0:T(1,128)S(1)}, f32[1,1536]{1,0:T(1,128)S(1)}, u32[]{:S(2)}, u32[]{:S(2)}) %collective-permute-start.6) | collective-permute-done | bytes 6176 | tf_op jit(solution)/shard_map/ppermute | solution.py:341
  28.1 0.8 %collective-permute-done.8.both = f32[1,1536]{1,0:T(1,128)S(1)} collective-permute-done((f32[1,1536]{1,0:T(1,128)S(1)}, f32[1,1536]{1,0:T(1,128)S(1)}, u32[]{:S(2)}, u32[]{:S(2)}) %collective-permute-start.8) | collective-permute-done | bytes 6176 | tf_op jit(solution)/shard_map/ppermute | solution.py:341
  32.3 7.5 %shard_map.140 = (bf16[128,2048]{1,0:T(8,128)(2,1)S(1)}, bf16[1792,3072]{1,0:T(8,128)(2,1)S(1)}) custom-call(bf16[16,6144]{1,0:T(8,128)(2,1)S(1)} %shard_map.136.refs_0_, bf16[16,6144]{1,0:T(8,128)(2,1)S(1)} %shard_map.137.refs_1_, bf16[16,6144]{1,0:T(8,128)(2,1)S(1)} %shard_map.138.refs_2_, bf16[16,6144]{1,0:T(8,128)(2,1)S(1)} %shard_map.139.refs_3_, ...), custom_call_target="tpu_custom_call" | custom-call | flops 6442450944 | bytes 11010048 | tf_op jit(solution)/shard_map/pallas_call | solution.py:312
  39.8 2.9 %shard_map.141 = (f32[64,3072]{1,0:T(8,128)S(1)}, bf16[64,3072]{1,0:T(8,128)(2,1)S(1)}, bf16[768,3072]{1,0:T(8,128)(2,1)S(1)}) custom-call(bf16[128,2048]{1,0:T(8,128)(2,1)S(1)} %get-tuple-element.45.hidden, bf16[1792,3072]{1,0:T(8,128)(2,1)S(1)} %get-tuple-element.46.ready, bf16[2048,6144]{1,0:T(8,128)(2,1)} %bitcast.19), custom_call_target="tpu_custom_call" | custom-call | flops 1610612736 | bytes 6291456 | tf_op jit(solution)/shard_map/pallas_call | solution.py:312
  43.0 3.7 %shard_map.142 = (f32[64,3072]{1,0:T(8,128)S(1)}, bf16[64,3072]{1,0:T(8,128)(2,1)S(1)}) custom-call(bf16[128,2048]{1,0:T(8,128)(2,1)S(1)} %get-tuple-element.45.hidden, bf16[768,3072]{1,0:T(8,128)(2,1)S(1)} %get-tuple-element.47.ready, bf16[2048,6144]{1,0:T(8,128)(2,1)} %bitcast.20), custom_call_target="tpu_custom_call" | custom-call | flops 1610612736 | bytes 7864320 | tf_op jit(solution)/shard_map/pallas_call | solution.py:312
  47.2 1.4 %collective-permute-start.24 = (bf16[16,3072]{1,0:T(8,128)(2,1)S(1)}, bf16[16,3072]{1,0:T(8,128)(2,1)S(1)}, u32[]{:S(2)}, u32[]{:S(2)}) collective-permute-start(bf16[16,3072]{1,0:T(8,128)(2,1)S(1)} %get-tuple-element.55), channel_id=1, source_target_pairs={{0,2},{1,3},{2,0},{3,1},{4,6},{5,7},{6,4},{7,5},{8,10},{9,11},{10,... | collective-permute-start | bytes 294920 | tf_op jit(solution)/shard_map/ppermute | solution.py:341
  49.3 1.3 %collective-permute-start.20 = (bf16[16,3072]{1,0:T(8,128)(2,1)S(1)}, bf16[16,3072]{1,0:T(8,128)(2,1)S(1)}, u32[]{:S(2)}, u32[]{:S(2)}) collective-permute-start(bf16[16,3072]{1,0:T(8,128)(2,1)S(1)} %get-tuple-element.53), channel_id=1, source_target_pairs={{0,2},{1,3},{2,0},{3,1},{4,6},{5,7},{6,4},{7,5},{8,10},{9,11},{10,... | collective-permute-start | bytes 294920 | tf_op jit(solution)/shard_map/ppermute | solution.py:341
  51.3 1.6 %collective-permute-done.24.crossed = bf16[16,3072]{1,0:T(8,128)(2,1)S(1)} collective-permute-done((bf16[16,3072]{1,0:T(8,128)(2,1)S(1)}, bf16[16,3072]{1,0:T(8,128)(2,1)S(1)}, u32[]{:S(2)}, u32[]{:S(2)}) %collective-permute-start.24) | collective-permute-done | bytes 98336 | tf_op jit(solution)/shard_map/ppermute | solution.py:341
  53.1 2.0 %collective-permute-done.22.crossed = bf16[16,3072]{1,0:T(8,128)(2,1)S(1)} collective-permute-done((bf16[16,3072]{1,0:T(8,128)(2,1)S(1)}, bf16[16,3072]{1,0:T(8,128)(2,1)S(1)}, u32[]{:S(2)}, u32[]{:S(2)}) %collective-permute-start.22) | collective-permute-done | bytes 98336 | tf_op jit(solution)/shard_map/ppermute | solution.py:341
  55.1 2.5 %collective-permute-start.23 = (bf16[16,3072]{1,0:T(8,128)(2,1)S(1)}, bf16[16,3072]{1,0:T(8,128)(2,1)S(1)}, u32[]{:S(2)}, u32[]{:S(2)}) collective-permute-start(bf16[16,3072]{1,0:T(8,128)(2,1)S(1)} %shard_map.146), channel_id=1, source_target_pairs={{0,16},{1,21},{2,18},{3,23},{4,20},{5,17},{6,22},{7,19},{8,24},{9,... | collective-permute-start | bytes 294920 | tf_op jit(solution)/shard_map/ppermute | solution.py:349
  59.2 1.3 %collective-permute-done.25.refs_3_ = bf16[16,3072]{1,0:T(8,128)(2,1)S(1)} collective-permute-done((bf16[16,3072]{1,0:T(8,128)(2,1)S(1)}, bf16[16,3072]{1,0:T(8,128)(2,1)S(1)}, u32[]{:S(2)}, u32[]{:S(2)}) %collective-permute-start.25) | collective-permute-done | bytes 98336 | tf_op jit(solution)/shard_map/ppermute | solution.py:349
  60.6 3.3 %collective-permute-done.23.refs_2_ = bf16[16,3072]{1,0:T(8,128)(2,1)S(1)} collective-permute-done((bf16[16,3072]{1,0:T(8,128)(2,1)S(1)}, bf16[16,3072]{1,0:T(8,128)(2,1)S(1)}, u32[]{:S(2)}, u32[]{:S(2)}) %collective-permute-start.23) | collective-permute-done | bytes 98336 | tf_op jit(solution)/shard_map/ppermute | solution.py:349
  64.7 4.0 %shard_map.131 = bf16[384,128]{1,0:T(8,128)(2,1)S(1)} custom-call(s32[32]{0:T(128)} %lengths_at.1, bf16[384,128]{1,0:T(8,128)(2,1)} %bitcast.21, bf16[32,2,128,128]{3,2,1,0:T(8,128)(2,1)} %k_at.1, bf16[32,2,128,128]{3,2,1,0:T(8,128)(2,1)} %v_at.1), custom_call_target="tpu_custom_call" | custom-call | flops 67108864 | bytes 4194304 | tf_op jit(solution)/shard_map/pallas_call | solution.py:312
  (81 shorter events, 11.6 us)
Async XLA Ops:
  0.6 4.1 %collective-permute-start = (bf16[32,1536]{1,0:T(8,128)(2,1)}, bf16[32,1536]{1,0:T(8,128)(2,1)S(1)}, u32[]{:S(2)}, u32[]{:S(2)}) collective-permute-start(bf16[32,1536]{1,0:T(8,128)(2,1)} %residual.1), channel_id=1, source_target_pairs={{0,1},{1,0},{2,3},{3,2},{4,5},{5,4},{6,7},{7,6},{8,9},{9,8},{10,11... | collective-permute-start | bytes 294920 | tf_op jit(solution)/shard_map/ppermute | solution.py:341
  1.2 6.2 %collective-permute-start.3 = (bf16[32,1536]{1,0:T(8,128)(2,1)}, bf16[32,1536]{1,0:T(8,128)(2,1)S(1)}, u32[]{:S(2)}, u32[]{:S(2)}) collective-permute-start(bf16[32,1536]{1,0:T(8,128)(2,1)} %residual.1), channel_id=1, source_target_pairs={{0,2},{1,3},{2,0},{3,1},{4,6},{5,7},{6,4},{7,5},{8,10},{9,11},{10,... | collective-permute-start | bytes 294920 | tf_op jit(solution)/shard_map/ppermute | solution.py:341
  7.3 4.2 %collective-permute-start.4 = (bf16[32,1536]{1,0:T(8,128)(2,1)S(1)}, bf16[32,1536]{1,0:T(8,128)(2,1)S(1)}, u32[]{:S(2)}, u32[]{:S(2)}) collective-permute-start(bf16[32,1536]{1,0:T(8,128)(2,1)S(1)} %collective-permute-done.3.refs_2_), channel_id=1, source_target_pairs={{0,1},{1,0},{2,3},{3,2},{4,5},{5,4},{6,7},{7,6},{8,9},{9,8},{10,11... | collective-permute-start | bytes 294920 | tf_op jit(solution)/shard_map/ppermute | solution.py:341
  7.7 7.0 %collective-permute-start.10 = (bf16[16,3072]{1,0:T(8,128)(2,1)S(1)}, bf16[16,3072]{1,0:T(8,128)(2,1)S(1)}, u32[]{:S(2)}, u32[]{:S(2)}) collective-permute-start(bf16[16,3072]{1,0:T(8,128)(2,1)S(1)} %get-tuple-element.44), channel_id=1, source_target_pairs={{0,24},{1,29},{2,26},{3,31},{4,28},{5,25},{6,30},{7,27},{8,16},{9,... | collective-permute-start | bytes 294920 | tf_op jit(solution)/shard_map/ppermute | solution.py:349
  11.8 17.7 %collective-permute-start.9 = (bf16[16,6144]{1,0:T(8,128)(2,1)S(1)}, bf16[16,6144]{1,0:T(8,128)(2,1)S(1)}, u32[]{:S(2)}, u32[]{:S(2)}) collective-permute-start(bf16[16,6144]{1,0:T(8,128)(2,1)S(1)} %get-tuple-element.40), channel_id=1, source_target_pairs={{0,8},{1,13},{2,10},{3,15},{4,12},{5,9},{6,14},{7,11},{8,0},{9,5},... | collective-permute-start | bytes 589832 | tf_op jit(solution)/shard_map/ppermute | solution.py:349
  11.9 17.8 %collective-permute-start.5 = (bf16[16,6144]{1,0:T(8,128)(2,1)S(1)}, bf16[16,6144]{1,0:T(8,128)(2,1)S(1)}, u32[]{:S(2)}, u32[]{:S(2)}) collective-permute-start(bf16[16,6144]{1,0:T(8,128)(2,1)S(1)} %get-tuple-element.37), channel_id=1, source_target_pairs={{0,0},{1,5},{2,2},{3,7},{4,4},{5,1},{6,6},{7,3},{8,8},{9,13},{10,1... | collective-permute-start | bytes 589832 | tf_op jit(solution)/shard_map/ppermute | solution.py:349
  12.7 7.9 %collective-permute-start.1 = (bf16[16,3072]{1,0:T(8,128)(2,1)S(1)}, bf16[16,3072]{1,0:T(8,128)(2,1)S(1)}, u32[]{:S(2)}, u32[]{:S(2)}) collective-permute-start(bf16[16,3072]{1,0:T(8,128)(2,1)S(1)} %get-tuple-element.36), channel_id=1, source_target_pairs={{0,16},{1,21},{2,18},{3,23},{4,20},{5,17},{6,22},{7,19},{8,24},{9,... | collective-permute-start | bytes 294920 | tf_op jit(solution)/shard_map/ppermute | solution.py:349
  14.6 14.3 %collective-permute-start.11 = (bf16[16,3072]{1,0:T(8,128)(2,1)S(1)}, bf16[16,3072]{1,0:T(8,128)(2,1)S(1)}, u32[]{:S(2)}, u32[]{:S(2)}) collective-permute-start(bf16[16,3072]{1,0:T(8,128)(2,1)S(1)} %collective-permute-done.10.refs_0_), channel_id=1, source_target_pairs={{0,2},{1,3},{2,0},{3,1},{4,6},{5,7},{6,4},{7,5},{8,10},{9,11},{10,... | collective-permute-start | bytes 294920 | tf_op jit(solution)/shard_map/ppermute | solution.py:341
  20.7 9.3 %collective-permute-start.2 = (bf16[16,3072]{1,0:T(8,128)(2,1)S(1)}, bf16[16,3072]{1,0:T(8,128)(2,1)S(1)}, u32[]{:S(2)}, u32[]{:S(2)}) collective-permute-start(bf16[16,3072]{1,0:T(8,128)(2,1)S(1)} %collective-permute-done.1.refs_0_), channel_id=1, source_target_pairs={{0,2},{1,3},{2,0},{3,1},{4,6},{5,7},{6,4},{7,5},{8,10},{9,11},{10,... | collective-permute-start | bytes 294920 | tf_op jit(solution)/shard_map/ppermute | solution.py:341
  22.1 3.6 %collective-permute-start.7 = (f32[1,1536]{1,0:T(1,128)S(1)}, f32[1,1536]{1,0:T(1,128)S(1)}, u32[]{:S(2)}, u32[]{:S(2)}) collective-permute-start(f32[1,1536]{1,0:T(1,128)S(1)} %broadcast_in_dim.3.own), channel_id=1, source_target_pairs={{0,2},{1,3},{2,0},{3,1},{4,6},{5,7},{6,4},{7,5},{8,10},{9,11},{10,... | collective-permute-start | bytes 18440 | tf_op jit(solution)/shard_map/ppermute | solution.py:341
  25.8 2.0 %collective-permute-start.6 = (f32[1,1536]{1,0:T(1,128)S(1)}, f32[1,1536]{1,0:T(1,128)S(1)}, u32[]{:S(2)}, u32[]{:S(2)}) collective-permute-start(f32[1,1536]{1,0:T(1,128)S(1)} %broadcast_in_dim.3.own), channel_id=1, source_target_pairs={{0,1},{1,0},{2,3},{3,2},{4,5},{5,4},{6,7},{7,6},{8,9},{9,8},{10,11... | collective-permute-start | bytes 18440 | tf_op jit(solution)/shard_map/ppermute | solution.py:341
  29.1 1.7 %collective-permute-start.15 = (bf16[16,6144]{1,0:T(8,128)(2,1)S(1)}, bf16[16,6144]{1,0:T(8,128)(2,1)S(1)}, u32[]{:S(2)}, u32[]{:S(2)}) collective-permute-start(bf16[16,6144]{1,0:T(8,128)(2,1)S(1)} %shard_map.139.refs_3_), channel_id=1, source_target_pairs={{0,1},{1,0},{2,3},{3,2},{4,5},{5,4},{6,7},{7,6},{8,9},{9,8},{10,11... | collective-permute-start | bytes 589832 | tf_op jit(solution)/shard_map/ppermute | solution.py:341
  30.4 1.6 %collective-permute-start.12 = (bf16[16,6144]{1,0:T(8,128)(2,1)S(1)}, bf16[16,6144]{1,0:T(8,128)(2,1)S(1)}, u32[]{:S(2)}, u32[]{:S(2)}) collective-permute-start(bf16[16,6144]{1,0:T(8,128)(2,1)S(1)} %shard_map.136.refs_0_), channel_id=1, source_target_pairs={{0,1},{1,0},{2,3},{3,2},{4,5},{5,4},{6,7},{7,6},{8,9},{9,8},{10,11... | collective-permute-start | bytes 589832 | tf_op jit(solution)/shard_map/ppermute | solution.py:341
  42.7 4.4 %collective-permute-start.17 = (bf16[64,3072]{1,0:T(8,128)(2,1)S(1)}, bf16[64,3072]{1,0:T(8,128)(2,1)S(1)}, u32[]{:S(2)}, u32[]{:S(2)}) collective-permute-start(bf16[64,3072]{1,0:T(8,128)(2,1)S(1)} %get-tuple-element.51), channel_id=1, source_target_pairs={{0,1},{1,0},{2,3},{3,2},{4,5},{5,4},{6,7},{7,6},{8,9},{9,8},{10,11... | collective-permute-start | bytes 1179656 | tf_op jit(solution)/shard_map/ppermute | solution.py:341
  46.8 4.5 %collective-permute-start.16 = (bf16[64,3072]{1,0:T(8,128)(2,1)S(1)}, bf16[64,3072]{1,0:T(8,128)(2,1)S(1)}, u32[]{:S(2)}, u32[]{:S(2)}) collective-permute-start(bf16[64,3072]{1,0:T(8,128)(2,1)S(1)} %get-tuple-element.49), channel_id=1, source_target_pairs={{0,1},{1,0},{2,3},{3,2},{4,5},{5,4},{6,7},{7,6},{8,9},{9,8},{10,11... | collective-permute-start | bytes 1179656 | tf_op jit(solution)/shard_map/ppermute | solution.py:341
  47.2 5.7 %collective-permute-start.24 = (bf16[16,3072]{1,0:T(8,128)(2,1)S(1)}, bf16[16,3072]{1,0:T(8,128)(2,1)S(1)}, u32[]{:S(2)}, u32[]{:S(2)}) collective-permute-start(bf16[16,3072]{1,0:T(8,128)(2,1)S(1)} %get-tuple-element.55), channel_id=1, source_target_pairs={{0,2},{1,3},{2,0},{3,1},{4,6},{5,7},{6,4},{7,5},{8,10},{9,11},{10,... | collective-permute-start | bytes 294920 | tf_op jit(solution)/shard_map/ppermute | solution.py:341
  48.6 6.4 %collective-permute-start.22 = (bf16[16,3072]{1,0:T(8,128)(2,1)S(1)}, bf16[16,3072]{1,0:T(8,128)(2,1)S(1)}, u32[]{:S(2)}, u32[]{:S(2)}) collective-permute-start(bf16[16,3072]{1,0:T(8,128)(2,1)S(1)} %get-tuple-element.54), channel_id=1, source_target_pairs={{0,2},{1,3},{2,0},{3,1},{4,6},{5,7},{6,4},{7,5},{8,10},{9,11},{10,... | collective-permute-start | bytes 294920 | tf_op jit(solution)/shard_map/ppermute | solution.py:341
  49.3 8.3 %collective-permute-start.20 = (bf16[16,3072]{1,0:T(8,128)(2,1)S(1)}, bf16[16,3072]{1,0:T(8,128)(2,1)S(1)}, u32[]{:S(2)}, u32[]{:S(2)}) collective-permute-start(bf16[16,3072]{1,0:T(8,128)(2,1)S(1)} %get-tuple-element.53), channel_id=1, source_target_pairs={{0,2},{1,3},{2,0},{3,1},{4,6},{5,7},{6,4},{7,5},{8,10},{9,11},{10,... | collective-permute-start | bytes 294920 | tf_op jit(solution)/shard_map/ppermute | solution.py:341
  50.6 7.9 %collective-permute-start.18 = (bf16[16,3072]{1,0:T(8,128)(2,1)S(1)}, bf16[16,3072]{1,0:T(8,128)(2,1)S(1)}, u32[]{:S(2)}, u32[]{:S(2)}) collective-permute-start(bf16[16,3072]{1,0:T(8,128)(2,1)S(1)} %get-tuple-element.52), channel_id=1, source_target_pairs={{0,2},{1,3},{2,0},{3,1},{4,6},{5,7},{6,4},{7,5},{8,10},{9,11},{10,... | collective-permute-start | bytes 294920 | tf_op jit(solution)/shard_map/ppermute | solution.py:341
  53.0 7.6 %collective-permute-start.25 = (bf16[16,3072]{1,0:T(8,128)(2,1)S(1)}, bf16[16,3072]{1,0:T(8,128)(2,1)S(1)}, u32[]{:S(2)}, u32[]{:S(2)}) collective-permute-start(bf16[16,3072]{1,0:T(8,128)(2,1)S(1)} %shard_map.147), channel_id=1, source_target_pairs={{0,24},{1,29},{2,26},{3,31},{4,28},{5,25},{6,30},{7,27},{8,16},{9,... | collective-permute-start | bytes 294920 | tf_op jit(solution)/shard_map/ppermute | solution.py:349
  55.1 8.8 %collective-permute-start.23 = (bf16[16,3072]{1,0:T(8,128)(2,1)S(1)}, bf16[16,3072]{1,0:T(8,128)(2,1)S(1)}, u32[]{:S(2)}, u32[]{:S(2)}) collective-permute-start(bf16[16,3072]{1,0:T(8,128)(2,1)S(1)} %shard_map.146), channel_id=1, source_target_pairs={{0,16},{1,21},{2,18},{3,23},{4,20},{5,17},{6,22},{7,19},{8,24},{9,... | collective-permute-start | bytes 294920 | tf_op jit(solution)/shard_map/ppermute | solution.py:349
  57.6 6.3 %collective-permute-start.21 = (bf16[16,3072]{1,0:T(8,128)(2,1)S(1)}, bf16[16,3072]{1,0:T(8,128)(2,1)S(1)}, u32[]{:S(2)}, u32[]{:S(2)}) collective-permute-start(bf16[16,3072]{1,0:T(8,128)(2,1)S(1)} %shard_map.145), channel_id=1, source_target_pairs={{0,8},{1,13},{2,10},{3,15},{4,12},{5,9},{6,14},{7,11},{8,0},{9,5},... | collective-permute-start | bytes 294920 | tf_op jit(solution)/shard_map/ppermute | solution.py:349
  58.6 5.4 %collective-permute-start.19 = (bf16[16,3072]{1,0:T(8,128)(2,1)S(1)}, bf16[16,3072]{1,0:T(8,128)(2,1)S(1)}, u32[]{:S(2)}, u32[]{:S(2)}) collective-permute-start(bf16[16,3072]{1,0:T(8,128)(2,1)S(1)} %shard_map.144), channel_id=1, source_target_pairs={{0,0},{1,5},{2,2},{3,7},{4,4},{5,1},{6,6},{7,3},{8,8},{9,13},{10,1... | collective-permute-start | bytes 294920 | tf_op jit(solution)/shard_map/ppermute | solution.py:349
  64.5 4.8 %collective-permute-start.26 = (f32[32,1536]{1,0:T(8,128)S(1)}, f32[32,1536]{1,0:T(8,128)S(1)}, u32[]{:S(2)}, u32[]{:S(2)}) collective-permute-start(f32[32,1536]{1,0:T(8,128)S(1)} %get-tuple-element.57), channel_id=1, source_target_pairs={{0,1},{1,0},{2,3},{3,2},{4,5},{5,4},{6,7},{7,6},{8,9},{9,8},{10,11... | collective-permute-start | bytes 589832 | tf_op jit(solution)/shard_map/ppermute | solution.py:341
  (17 other events, 304.6 us)

commit v2 on v0

--- a/solution.py
+++ b/solution.py
@@ -11,7 +11,7 @@
 TOP = 2
 WIDE = 512
 DEEP = 256
-EARLY = 6
+EARLY = 7
 LATER = 3
 VMEM_ROWS = 128
 ROUTE_FLOPS = 2e10
@@ -40,36 +40,29 @@
     return context.astype(jnp.bfloat16).reshape(seq_count, head_count, head_size)
 
 
-def attend_kernel(scale, seqs, lengths_at, q_at, k_at, v_at, out, lengths, q, k, v, wide, score, prob, sems):
-    copies = [
+def attend_kernel(scale, seqs, lengths_at, q_at, k, v, out, lengths, q, wide, score, prob, sems):
+    near = [
         pltpu.make_async_copy(source, target, sems.at[i])
-        for i, (source, target) in enumerate(
-            ((lengths_at, lengths), (q_at, q), (k_at, k), (v_at, v))
-        )
+        for i, (source, target) in enumerate(((lengths_at, lengths), (q_at, q)))
     ]
-    for copy in copies:
+    for copy in near:
         copy.start()
     heads, size = q.shape[0] // seqs, q.shape[1]
-    kv = k.shape[1]
+    kv, positions = k.shape[1], k.shape[2]
     tall = wide.shape[0] // seqs
     group = heads // kv
-    positions = k.shape[2]
     row = lax.broadcasted_iota(jnp.int32, (tall, positions), 0)
     lane = lax.broadcasted_iota(jnp.int32, (tall, positions), 1)
-    copies[0].wait()
-    copies[1].wait()
+    for copy in near:
+        copy.wait()
     wide[: heads * seqs, :] = q[...].astype(jnp.float32)
     wide[heads * seqs :, :] = jnp.zeros(((tall - heads) * seqs, size), jnp.float32)
-    copies[2].wait()
     for b in range(seqs):
         queries = wide[pl.ds(b, tall, stride=seqs), :].astype(jnp.bfloat16)
         total = None
         for j in range(kv):
             dots = lax.dot_general(
-                queries,
-                k[b, j],
-                (((1,), (1,)), ((), ())),
-                preferred_element_type=jnp.float32,
+                queries, k[b, j], (((1,), (1,)), ((), ())), preferred_element_type=jnp.float32
             )
             total = dots if total is None else jnp.where(row < j * group, total, dots)
         live = lane < lengths[b]
@@ -77,7 +70,6 @@
     top = jnp.max(score[...], axis=-1, keepdims=True)
     expo = jnp.exp(score[...] - top)
     prob[...] = (expo / jnp.sum(expo, axis=-1, keepdims=True)).astype(jnp.bfloat16)
-    copies[3].wait()
     for b in range(seqs):
         probs = prob[b * tall : (b + 1) * tall, :].astype(jnp.float32)
         total = jnp.zeros((tall, size), jnp.float32)
@@ -345,7 +337,9 @@
         flops=ROUTE_FLOPS,
         moved=1e5,
     )
-    gain, sibling, select = lax.optimization_barrier((norm_gain[None, :], sibling, select))
+    gain, select = lax.optimization_barrier((norm_gain, select))
+    gain = gain[None, :]
+    gain, sibling, select = lax.optimization_barrier((gain, sibling, select))
 
     def pack(first, count, total, sources):
         return call(
@@ -374,18 +368,22 @@
         [held(1, depth, dtype=f32)],
     )
 
-    normed = []
-    for k in order:
-        parts = [full[k]] if k < low else [near[k - low], across(near[k - low], 2)]
-        normed += call(
+    def norm(parts):
+        return call(
             norm_kernel,
             [*parts, gains],
             [IN_VMEM] * (len(parts) + 1),
             [held(slots, depth)],
             flops=8 * slots * depth,
             moved=4 * slots * depth,
-        )
-    entering = [in_vmem(v) for v in normed + [across(v, 1) for v in normed]]
+        )[0]
+
+    normed = [norm([part]) for part in full]
+    far = [across(part, 2) for part in near]
+    far[:-1], normed = lax.optimization_barrier((far[:-1], normed))
+    normed += [norm([here, there]) for here, there in zip(near, far)]
+    traded = [across(v, 1) for v in normed]
+    entering = [in_vmem(v) for v in normed + traded]
     blocks = hid // DEEP
     early, later = min(EARLY, blocks - 1), min(LATER, blocks - 1)
     weight = in_hbm(w_down[0])
@@ -518,20 +516,18 @@
     positions = k_cache.shape[2]
     (out,) = call(
         functools.partial(attend_kernel, size ** (-0.5), seqs),
-        [in_hbm(v) for v in (lengths, flat, k_cache, v_cache)],
-        [IN_PLACE] * 4,
+        [in_hbm(lengths), in_hbm(flat), in_vmem(k_cache), in_vmem(v_cache)],
+        [IN_PLACE] * 2 + [IN_VMEM] * 2,
         [held(heads * seqs, size)],
         scratch=[
             pltpu.SMEM(lengths.shape, jnp.int32),
             pltpu.VMEM(flat.shape, flat.dtype),
-            pltpu.VMEM(k_cache.shape, k_cache.dtype),
-            pltpu.VMEM(v_cache.shape, v_cache.dtype),
             pltpu.VMEM((tall * seqs, size), jnp.float32),
             pltpu.VMEM((tall * seqs, positions), jnp.float32),
             pltpu.VMEM((tall * seqs, positions), jnp.bfloat16),
-            pltpu.SemaphoreType.DMA((4,)),
+            pltpu.SemaphoreType.DMA((2,)),
         ],
-        mib=7,
+        mib=3,
         flops=8 * seqs * tall * size * positions,
         moved=2 * k_cache.size * 2,
     )

time: 70.2 us -> 69 us (0.983)
  waiting for transfers between devices: 15 us -> 22.3 us
  starting transfers between devices: 31.5 us -> 24.3 us
  Pallas kernels: 21.2 us -> 19.8 us
    ppermute x8, waiting for transfers between devices: 4.75 us -> 9.21 us  [between(): return lax.ppermute(v, ('expert', 'mp'), pairs)]
    ppermute x8, starting transfers between devices: 13.7 us -> 9.66 us  [between(): return lax.ppermute(v, ('expert', 'mp'), pairs)]
    ppermute x19, starting transfers between devices: 17.8 us -> 14.6 us  [across(): return lax.ppermute(v, 'mp', [(i, i ^ bit) for i in range(members)])]
    ppermute x19, waiting for transfers between devices: 10.3 us -> 13 us  [across(): return lax.ppermute(v, 'mp', [(i, i ^ bit) for i in range(members)])]
    pallas_call x18, Pallas kernels: 21.2 us -> 19.8 us  [call(): pl.pallas_call(body, out_shape=outs, in_specs=specs, out_specs=[IN_VMEM]...]
  transfers between devices with their start and end apart: 27 -> 27, of which waited for: 11 -> 15; matrix products, arithmetic and copies ran while one was open for 1% -> 1% of each run, Pallas kernels for 14% -> 13%
where the time goes in v2:
time: 69 us; the launch traced here: 68.8 us
  starting transfers between devices  24.3 us (35%)
  waiting for transfers between devices  22.3 us (32%)
  Pallas kernels  19.8 us (29%)
  between operations  1.03 us (1%)
  local copies, waits for them, and re-layouts  0.73 us (1%)
    pallas_call x18, Pallas kernels, call(): pl.pallas_call(body, out_shape=outs, in_specs=specs, out_specs=[IN_VMEM]...  19.8 us
    ppermute x19, starting transfers between devices, across(): return lax.ppermute(v, 'mp', [(i, i ^ bit) for i in range(members)])  14.6 us
    ppermute x19, waiting for transfers between devices, across(): return lax.ppermute(v, 'mp', [(i, i ^ bit) for i in range(members)])  13 us
    ppermute x8, starting transfers between devices, between(): return lax.ppermute(v, ('expert', 'mp'), pairs)  9.66 us
    ppermute x8, waiting for transfers between devices, between(): return lax.ppermute(v, ('expert', 'mp'), pairs)  9.21 us
  transfers between devices with their start and end apart: 27, of which 15 were waited for; matrix products, arithmetic and copies ran while one was open for 1% of the time, Pallas kernels for 13%

profile of v2, /device:TPU:0, one launch (start us, length us, event | category | flops | bytes accessed | tf_op | source)
XLA Modules:
  0.0 68.8 jit_solution(4970756532255184876)
XLA Ops:
  1.2 2.6 %collective-permute-start.3 = (bf16[32,1536]{1,0:T(8,128)(2,1)}, bf16[32,1536]{1,0:T(8,128)(2,1)S(1)}, u32[]{:S(2)}, u32[]{:S(2)}) collective-permute-start(bf16[32,1536]{1,0:T(8,128)(2,1)} %residual.1), channel_id=1, source_target_pairs={{0,2},{1,3},{2,0},{3,1},{4,6},{5,7},{6,4},{7,5},{8,10},{9,11},{10,... | collective-permute-start | bytes 294920 | tf_op jit(solution)/shard_map/ppermute | solution.py:313
  3.7 1.0 %shard_map.132 = (bf16[64,32]{1,0:T(8,128)(2,1)S(1)}, f32[64,32]{1,0:T(8,128)S(1)}) custom-call(s32[2,32]{1,0:T(2,128)} %bitcast.22, f32[2,32]{1,0:T(2,128)} %bitcast.23, s32[8]{0:T(128)} %cap_at.1), custom_call_target="tpu_custom_call" | custom-call | flops 20000000000 | bytes 100000 | tf_op jit(solution)/shard_map/pallas_call | solution.py:284
  4.8 2.6 %collective-permute-done.3.refs_2_ = bf16[32,1536]{1,0:T(8,128)(2,1)S(1)} collective-permute-done((bf16[32,1536]{1,0:T(8,128)(2,1)}, bf16[32,1536]{1,0:T(8,128)(2,1)S(1)}, u32[]{:S(2)}, u32[]{:S(2)}) %collective-permute-start.3) | collective-permute-done | bytes 98336 | tf_op jit(solution)/shard_map/ppermute | solution.py:313
  7.7 3.9 %collective-permute-start.10 = (bf16[16,3072]{1,0:T(8,128)(2,1)S(1)}, bf16[16,3072]{1,0:T(8,128)(2,1)S(1)}, u32[]{:S(2)}, u32[]{:S(2)}) collective-permute-start(bf16[16,3072]{1,0:T(8,128)(2,1)S(1)} %get-tuple-element.44), channel_id=1, source_target_pairs={{0,24},{1,29},{2,26},{3,31},{4,28},{5,25},{6,30},{7,27},{8,16},{9,... | collective-permute-start | bytes 294920 | tf_op jit(solution)/shard_map/ppermute | solution.py:321
  11.9 0.8 %collective-permute-start.5 = (bf16[16,6144]{1,0:T(8,128)(2,1)S(1)}, bf16[16,6144]{1,0:T(8,128)(2,1)S(1)}, u32[]{:S(2)}, u32[]{:S(2)}) collective-permute-start(bf16[16,6144]{1,0:T(8,128)(2,1)S(1)} %get-tuple-element.37), channel_id=1, source_target_pairs={{0,0},{1,5},{2,2},{3,7},{4,4},{5,1},{6,6},{7,3},{8,8},{9,13},{10,1... | collective-permute-start | bytes 589832 | tf_op jit(solution)/shard_map/ppermute | solution.py:321
  12.7 1.5 %collective-permute-start.1 = (bf16[16,3072]{1,0:T(8,128)(2,1)S(1)}, bf16[16,3072]{1,0:T(8,128)(2,1)S(1)}, u32[]{:S(2)}, u32[]{:S(2)}) collective-permute-start(bf16[16,3072]{1,0:T(8,128)(2,1)S(1)} %get-tuple-element.36), channel_id=1, source_target_pairs={{0,16},{1,21},{2,18},{3,23},{4,20},{5,17},{6,22},{7,19},{8,24},{9,... | collective-permute-start | bytes 294920 | tf_op jit(solution)/shard_map/ppermute | solution.py:321
  14.6 1.9 %collective-permute-start.11 = (bf16[16,3072]{1,0:T(8,128)(2,1)S(1)}, bf16[16,3072]{1,0:T(8,128)(2,1)S(1)}, u32[]{:S(2)}, u32[]{:S(2)}) collective-permute-start(bf16[16,3072]{1,0:T(8,128)(2,1)S(1)} %collective-permute-done.10.refs_0_), channel_id=1, source_target_pairs={{0,2},{1,3},{2,0},{3,1},{4,6},{5,7},{6,4},{7,5},{8,10},{9,11},{10,... | collective-permute-start | bytes 294920 | tf_op jit(solution)/shard_map/ppermute | solution.py:313
  16.5 4.1 %collective-permute-done.1.refs_0_ = bf16[16,3072]{1,0:T(8,128)(2,1)S(1)} collective-permute-done((bf16[16,3072]{1,0:T(8,128)(2,1)S(1)}, bf16[16,3072]{1,0:T(8,128)(2,1)S(1)}, u32[]{:S(2)}, u32[]{:S(2)}) %collective-permute-start.1) | collective-permute-done | bytes 98336 | tf_op jit(solution)/shard_map/ppermute | solution.py:321
  20.7 1.5 %collective-permute-start.2 = (bf16[16,3072]{1,0:T(8,128)(2,1)S(1)}, bf16[16,3072]{1,0:T(8,128)(2,1)S(1)}, u32[]{:S(2)}, u32[]{:S(2)}) collective-permute-start(bf16[16,3072]{1,0:T(8,128)(2,1)S(1)} %collective-permute-done.1.refs_0_), channel_id=1, source_target_pairs={{0,2},{1,3},{2,0},{3,1},{4,6},{5,7},{6,4},{7,5},{8,10},{9,11},{10,... | collective-permute-start | bytes 294920 | tf_op jit(solution)/shard_map/ppermute | solution.py:313
  22.7 3.1 %collective-permute-done.7.across = f32[1,1536]{1,0:T(1,128)S(1)} collective-permute-done((f32[1,1536]{1,0:T(1,128)S(1)}, f32[1,1536]{1,0:T(1,128)S(1)}, u32[]{:S(2)}, u32[]{:S(2)}) %collective-permute-start.7) | collective-permute-done | bytes 6176 | tf_op jit(solution)/shard_map/ppermute | solution.py:313
  25.8 1.2 %collective-permute-start.6 = (f32[1,1536]{1,0:T(1,128)S(1)}, f32[1,1536]{1,0:T(1,128)S(1)}, u32[]{:S(2)}, u32[]{:S(2)}) collective-permute-start(f32[1,1536]{1,0:T(1,128)S(1)} %broadcast_in_dim.3.own), channel_id=1, source_target_pairs={{0,1},{1,0},{2,3},{3,2},{4,5},{5,4},{6,7},{7,6},{8,9},{9,8},{10,11... | collective-permute-start | bytes 18440 | tf_op jit(solution)/shard_map/ppermute | solution.py:313
  26.9 0.8 %collective-permute-done.6.sibling = f32[1,1536]{1,0:T(1,128)S(1)} collective-permute-done((f32[1,1536]{1,0:T(1,128)S(1)}, f32[1,1536]{1,0:T(1,128)S(1)}, u32[]{:S(2)}, u32[]{:S(2)}) %collective-permute-start.6) | collective-permute-done | bytes 6176 | tf_op jit(solution)/shard_map/ppermute | solution.py:313
  28.1 0.8 %collective-permute-done.8.both = f32[1,1536]{1,0:T(1,128)S(1)} collective-permute-done((f32[1,1536]{1,0:T(1,128)S(1)}, f32[1,1536]{1,0:T(1,128)S(1)}, u32[]{:S(2)}, u32[]{:S(2)}) %collective-permute-start.8) | collective-permute-done | bytes 6176 | tf_op jit(solution)/shard_map/ppermute | solution.py:313
  32.3 7.5 %shard_map.140 = (bf16[128,2048]{1,0:T(8,128)(2,1)S(1)}, bf16[1792,3072]{1,0:T(8,128)(2,1)S(1)}) custom-call(bf16[16,6144]{1,0:T(8,128)(2,1)S(1)} %shard_map.136.refs_0_, bf16[16,6144]{1,0:T(8,128)(2,1)S(1)} %shard_map.137.refs_1_, bf16[16,6144]{1,0:T(8,128)(2,1)S(1)} %shard_map.138.refs_2_, bf16[16,6144]{1,0:T(8,128)(2,1)S(1)} %shard_map.139.refs_3_, ...), custom_call_target="tpu_custom_call" | custom-call | flops 6442450944 | bytes 11010048 | tf_op jit(solution)/shard_map/pallas_call | solution.py:284
  39.8 2.9 %shard_map.141 = (f32[64,3072]{1,0:T(8,128)S(1)}, bf16[64,3072]{1,0:T(8,128)(2,1)S(1)}, bf16[768,3072]{1,0:T(8,128)(2,1)S(1)}) custom-call(bf16[128,2048]{1,0:T(8,128)(2,1)S(1)} %get-tuple-element.45.hidden, bf16[1792,3072]{1,0:T(8,128)(2,1)S(1)} %get-tuple-element.46.ready, bf16[2048,6144]{1,0:T(8,128)(2,1)} %bitcast.19), custom_call_target="tpu_custom_call" | custom-call | flops 1610612736 | bytes 6291456 | tf_op jit(solution)/shard_map/pallas_call | solution.py:284
  43.0 3.9 %shard_map.142 = (f32[64,3072]{1,0:T(8,128)S(1)}, bf16[64,3072]{1,0:T(8,128)(2,1)S(1)}) custom-call(bf16[128,2048]{1,0:T(8,128)(2,1)S(1)} %get-tuple-element.45.hidden, bf16[768,3072]{1,0:T(8,128)(2,1)S(1)} %get-tuple-element.47.ready, bf16[2048,6144]{1,0:T(8,128)(2,1)} %bitcast.20), custom_call_target="tpu_custom_call" | custom-call | flops 1610612736 | bytes 7864320 | tf_op jit(solution)/shard_map/pallas_call | solution.py:284
  47.4 1.4 %collective-permute-start.24 = (bf16[16,3072]{1,0:T(8,128)(2,1)S(1)}, bf16[16,3072]{1,0:T(8,128)(2,1)S(1)}, u32[]{:S(2)}, u32[]{:S(2)}) collective-permute-start(bf16[16,3072]{1,0:T(8,128)(2,1)S(1)} %get-tuple-element.55), channel_id=1, source_target_pairs={{0,2},{1,3},{2,0},{3,1},{4,6},{5,7},{6,4},{7,5},{8,10},{9,11},{10,... | collective-permute-start | bytes 294920 | tf_op jit(solution)/shard_map/ppermute | solution.py:313
  49.5 1.3 %collective-permute-start.20 = (bf16[16,3072]{1,0:T(8,128)(2,1)S(1)}, bf16[16,3072]{1,0:T(8,128)(2,1)S(1)}, u32[]{:S(2)}, u32[]{:S(2)}) collective-permute-start(bf16[16,3072]{1,0:T(8,128)(2,1)S(1)} %get-tuple-element.53), channel_id=1, source_target_pairs={{0,2},{1,3},{2,0},{3,1},{4,6},{5,7},{6,4},{7,5},{8,10},{9,11},{10,... | collective-permute-start | bytes 294920 | tf_op jit(solution)/shard_map/ppermute | solution.py:313
  51.5 1.6 %collective-permute-done.24.crossed = bf16[16,3072]{1,0:T(8,128)(2,1)S(1)} collective-permute-done((bf16[16,3072]{1,0:T(8,128)(2,1)S(1)}, bf16[16,3072]{1,0:T(8,128)(2,1)S(1)}, u32[]{:S(2)}, u32[]{:S(2)}) %collective-permute-start.24) | collective-permute-done | bytes 98336 | tf_op jit(solution)/shard_map/ppermute | solution.py:313
  53.2 2.0 %collective-permute-done.22.crossed = bf16[16,3072]{1,0:T(8,128)(2,1)S(1)} collective-permute-done((bf16[16,3072]{1,0:T(8,128)(2,1)S(1)}, bf16[16,3072]{1,0:T(8,128)(2,1)S(1)}, u32[]{:S(2)}, u32[]{:S(2)}) %collective-permute-start.22) | collective-permute-done | bytes 98336 | tf_op jit(solution)/shard_map/ppermute | solution.py:313
  55.2 2.5 %collective-permute-start.23 = (bf16[16,3072]{1,0:T(8,128)(2,1)S(1)}, bf16[16,3072]{1,0:T(8,128)(2,1)S(1)}, u32[]{:S(2)}, u32[]{:S(2)}) collective-permute-start(bf16[16,3072]{1,0:T(8,128)(2,1)S(1)} %shard_map.146), channel_id=1, source_target_pairs={{0,16},{1,21},{2,18},{3,23},{4,20},{5,17},{6,22},{7,19},{8,24},{9,... | collective-permute-start | bytes 294920 | tf_op jit(solution)/shard_map/ppermute | solution.py:321
  59.4 1.4 %collective-permute-done.25.refs_3_ = bf16[16,3072]{1,0:T(8,128)(2,1)S(1)} collective-permute-done((bf16[16,3072]{1,0:T(8,128)(2,1)S(1)}, bf16[16,3072]{1,0:T(8,128)(2,1)S(1)}, u32[]{:S(2)}, u32[]{:S(2)}) %collective-permute-start.25) | collective-permute-done | bytes 98336 | tf_op jit(solution)/shard_map/ppermute | solution.py:321
  60.8 3.2 %collective-permute-done.23.refs_2_ = bf16[16,3072]{1,0:T(8,128)(2,1)S(1)} collective-permute-done((bf16[16,3072]{1,0:T(8,128)(2,1)S(1)}, bf16[16,3072]{1,0:T(8,128)(2,1)S(1)}, u32[]{:S(2)}, u32[]{:S(2)}) %collective-permute-start.23) | collective-permute-done | bytes 98336 | tf_op jit(solution)/shard_map/ppermute | solution.py:321
  64.8 2.7 %shard_map.131 = bf16[384,128]{1,0:T(8,128)(2,1)S(1)} custom-call(s32[32]{0:T(128)} %lengths_at.1, bf16[384,128]{1,0:T(8,128)(2,1)} %bitcast.21, bf16[32,2,128,128]{3,2,1,0:T(8,128)(2,1)S(1)} %copy-done, bf16[32,2,128,128]{3,2,1,0:T(8,128)(2,1)S(1)} %copy-done.1), custom_call_target="tpu_custom_call" | custom-call | flops 67108864 | bytes 4194304 | tf_op jit(solution)/shard_map/pallas_call | solution.py:284
  (85 shorter events, 11.6 us)
Async XLA Ops:
  0.6 4.1 %collective-permute-start = (bf16[32,1536]{1,0:T(8,128)(2,1)}, bf16[32,1536]{1,0:T(8,128)(2,1)S(1)}, u32[]{:S(2)}, u32[]{:S(2)}) collective-permute-start(bf16[32,1536]{1,0:T(8,128)(2,1)} %residual.1), channel_id=1, source_target_pairs={{0,1},{1,0},{2,3},{3,2},{4,5},{5,4},{6,7},{7,6},{8,9},{9,8},{10,11... | collective-permute-start | bytes 294920 | tf_op jit(solution)/shard_map/ppermute | solution.py:313
  1.2 6.2 %collective-permute-start.3 = (bf16[32,1536]{1,0:T(8,128)(2,1)}, bf16[32,1536]{1,0:T(8,128)(2,1)S(1)}, u32[]{:S(2)}, u32[]{:S(2)}) collective-permute-start(bf16[32,1536]{1,0:T(8,128)(2,1)} %residual.1), channel_id=1, source_target_pairs={{0,2},{1,3},{2,0},{3,1},{4,6},{5,7},{6,4},{7,5},{8,10},{9,11},{10,... | collective-permute-start | bytes 294920 | tf_op jit(solution)/shard_map/ppermute | solution.py:313
  7.3 4.2 %collective-permute-start.4 = (bf16[32,1536]{1,0:T(8,128)(2,1)S(1)}, bf16[32,1536]{1,0:T(8,128)(2,1)S(1)}, u32[]{:S(2)}, u32[]{:S(2)}) collective-permute-start(bf16[32,1536]{1,0:T(8,128)(2,1)S(1)} %collective-permute-done.3.refs_2_), channel_id=1, source_target_pairs={{0,1},{1,0},{2,3},{3,2},{4,5},{5,4},{6,7},{7,6},{8,9},{9,8},{10,11... | collective-permute-start | bytes 294920 | tf_op jit(solution)/shard_map/ppermute | solution.py:313
  7.7 7.0 %collective-permute-start.10 = (bf16[16,3072]{1,0:T(8,128)(2,1)S(1)}, bf16[16,3072]{1,0:T(8,128)(2,1)S(1)}, u32[]{:S(2)}, u32[]{:S(2)}) collective-permute-start(bf16[16,3072]{1,0:T(8,128)(2,1)S(1)} %get-tuple-element.44), channel_id=1, source_target_pairs={{0,24},{1,29},{2,26},{3,31},{4,28},{5,25},{6,30},{7,27},{8,16},{9,... | collective-permute-start | bytes 294920 | tf_op jit(solution)/shard_map/ppermute | solution.py:321
  11.8 17.7 %collective-permute-start.9 = (bf16[16,6144]{1,0:T(8,128)(2,1)S(1)}, bf16[16,6144]{1,0:T(8,128)(2,1)S(1)}, u32[]{:S(2)}, u32[]{:S(2)}) collective-permute-start(bf16[16,6144]{1,0:T(8,128)(2,1)S(1)} %get-tuple-element.40), channel_id=1, source_target_pairs={{0,8},{1,13},{2,10},{3,15},{4,12},{5,9},{6,14},{7,11},{8,0},{9,5},... | collective-permute-start | bytes 589832 | tf_op jit(solution)/shard_map/ppermute | solution.py:321
  11.9 17.8 %collective-permute-start.5 = (bf16[16,6144]{1,0:T(8,128)(2,1)S(1)}, bf16[16,6144]{1,0:T(8,128)(2,1)S(1)}, u32[]{:S(2)}, u32[]{:S(2)}) collective-permute-start(bf16[16,6144]{1,0:T(8,128)(2,1)S(1)} %get-tuple-element.37), channel_id=1, source_target_pairs={{0,0},{1,5},{2,2},{3,7},{4,4},{5,1},{6,6},{7,3},{8,8},{9,13},{10,1... | collective-permute-start | bytes 589832 | tf_op jit(solution)/shard_map/ppermute | solution.py:321
  12.7 7.9 %collective-permute-start.1 = (bf16[16,3072]{1,0:T(8,128)(2,1)S(1)}, bf16[16,3072]{1,0:T(8,128)(2,1)S(1)}, u32[]{:S(2)}, u32[]{:S(2)}) collective-permute-start(bf16[16,3072]{1,0:T(8,128)(2,1)S(1)} %get-tuple-element.36), channel_id=1, source_target_pairs={{0,16},{1,21},{2,18},{3,23},{4,20},{5,17},{6,22},{7,19},{8,24},{9,... | collective-permute-start | bytes 294920 | tf_op jit(solution)/shard_map/ppermute | solution.py:321
  14.6 14.3 %collective-permute-start.11 = (bf16[16,3072]{1,0:T(8,128)(2,1)S(1)}, bf16[16,3072]{1,0:T(8,128)(2,1)S(1)}, u32[]{:S(2)}, u32[]{:S(2)}) collective-permute-start(bf16[16,3072]{1,0:T(8,128)(2,1)S(1)} %collective-permute-done.10.refs_0_), channel_id=1, source_target_pairs={{0,2},{1,3},{2,0},{3,1},{4,6},{5,7},{6,4},{7,5},{8,10},{9,11},{10,... | collective-permute-start | bytes 294920 | tf_op jit(solution)/shard_map/ppermute | solution.py:313
  20.7 9.3 %collective-permute-start.2 = (bf16[16,3072]{1,0:T(8,128)(2,1)S(1)}, bf16[16,3072]{1,0:T(8,128)(2,1)S(1)}, u32[]{:S(2)}, u32[]{:S(2)}) collective-permute-start(bf16[16,3072]{1,0:T(8,128)(2,1)S(1)} %collective-permute-done.1.refs_0_), channel_id=1, source_target_pairs={{0,2},{1,3},{2,0},{3,1},{4,6},{5,7},{6,4},{7,5},{8,10},{9,11},{10,... | collective-permute-start | bytes 294920 | tf_op jit(solution)/shard_map/ppermute | solution.py:313
  22.1 3.6 %collective-permute-start.7 = (f32[1,1536]{1,0:T(1,128)S(1)}, f32[1,1536]{1,0:T(1,128)S(1)}, u32[]{:S(2)}, u32[]{:S(2)}) collective-permute-start(f32[1,1536]{1,0:T(1,128)S(1)} %broadcast_in_dim.3.own), channel_id=1, source_target_pairs={{0,2},{1,3},{2,0},{3,1},{4,6},{5,7},{6,4},{7,5},{8,10},{9,11},{10,... | collective-permute-start | bytes 18440 | tf_op jit(solution)/shard_map/ppermute | solution.py:313
  25.8 2.0 %collective-permute-start.6 = (f32[1,1536]{1,0:T(1,128)S(1)}, f32[1,1536]{1,0:T(1,128)S(1)}, u32[]{:S(2)}, u32[]{:S(2)}) collective-permute-start(f32[1,1536]{1,0:T(1,128)S(1)} %broadcast_in_dim.3.own), channel_id=1, source_target_pairs={{0,1},{1,0},{2,3},{3,2},{4,5},{5,4},{6,7},{7,6},{8,9},{9,8},{10,11... | collective-permute-start | bytes 18440 | tf_op jit(solution)/shard_map/ppermute | solution.py:313
  29.1 1.7 %collective-permute-start.15 = (bf16[16,6144]{1,0:T(8,128)(2,1)S(1)}, bf16[16,6144]{1,0:T(8,128)(2,1)S(1)}, u32[]{:S(2)}, u32[]{:S(2)}) collective-permute-start(bf16[16,6144]{1,0:T(8,128)(2,1)S(1)} %shard_map.139.refs_3_), channel_id=1, source_target_pairs={{0,1},{1,0},{2,3},{3,2},{4,5},{5,4},{6,7},{7,6},{8,9},{9,8},{10,11... | collective-permute-start | bytes 589832 | tf_op jit(solution)/shard_map/ppermute | solution.py:313
  30.4 1.6 %collective-permute-start.12 = (bf16[16,6144]{1,0:T(8,128)(2,1)S(1)}, bf16[16,6144]{1,0:T(8,128)(2,1)S(1)}, u32[]{:S(2)}, u32[]{:S(2)}) collective-permute-start(bf16[16,6144]{1,0:T(8,128)(2,1)S(1)} %shard_map.136.refs_0_), channel_id=1, source_target_pairs={{0,1},{1,0},{2,3},{3,2},{4,5},{5,4},{6,7},{7,6},{8,9},{9,8},{10,11... | collective-permute-start | bytes 589832 | tf_op jit(solution)/shard_map/ppermute | solution.py:313
  42.7 4.5 %collective-permute-start.17 = (bf16[64,3072]{1,0:T(8,128)(2,1)S(1)}, bf16[64,3072]{1,0:T(8,128)(2,1)S(1)}, u32[]{:S(2)}, u32[]{:S(2)}) collective-permute-start(bf16[64,3072]{1,0:T(8,128)(2,1)S(1)} %get-tuple-element.51), channel_id=1, source_target_pairs={{0,1},{1,0},{2,3},{3,2},{4,5},{5,4},{6,7},{7,6},{8,9},{9,8},{10,11... | collective-permute-start | bytes 1179656 | tf_op jit(solution)/shard_map/ppermute | solution.py:313
  46.9 4.5 %collective-permute-start.16 = (bf16[64,3072]{1,0:T(8,128)(2,1)S(1)}, bf16[64,3072]{1,0:T(8,128)(2,1)S(1)}, u32[]{:S(2)}, u32[]{:S(2)}) collective-permute-start(bf16[64,3072]{1,0:T(8,128)(2,1)S(1)} %get-tuple-element.49), channel_id=1, source_target_pairs={{0,1},{1,0},{2,3},{3,2},{4,5},{5,4},{6,7},{7,6},{8,9},{9,8},{10,11... | collective-permute-start | bytes 1179656 | tf_op jit(solution)/shard_map/ppermute | solution.py:313
  47.4 5.7 %collective-permute-start.24 = (bf16[16,3072]{1,0:T(8,128)(2,1)S(1)}, bf16[16,3072]{1,0:T(8,128)(2,1)S(1)}, u32[]{:S(2)}, u32[]{:S(2)}) collective-permute-start(bf16[16,3072]{1,0:T(8,128)(2,1)S(1)} %get-tuple-element.55), channel_id=1, source_target_pairs={{0,2},{1,3},{2,0},{3,1},{4,6},{5,7},{6,4},{7,5},{8,10},{9,11},{10,... | collective-permute-start | bytes 294920 | tf_op jit(solution)/shard_map/ppermute | solution.py:313
  48.8 6.5 %collective-permute-start.22 = (bf16[16,3072]{1,0:T(8,128)(2,1)S(1)}, bf16[16,3072]{1,0:T(8,128)(2,1)S(1)}, u32[]{:S(2)}, u32[]{:S(2)}) collective-permute-start(bf16[16,3072]{1,0:T(8,128)(2,1)S(1)} %get-tuple-element.54), channel_id=1, source_target_pairs={{0,2},{1,3},{2,0},{3,1},{4,6},{5,7},{6,4},{7,5},{8,10},{9,11},{10,... | collective-permute-start | bytes 294920 | tf_op jit(solution)/shard_map/ppermute | solution.py:313
  49.5 8.3 %collective-permute-start.20 = (bf16[16,3072]{1,0:T(8,128)(2,1)S(1)}, bf16[16,3072]{1,0:T(8,128)(2,1)S(1)}, u32[]{:S(2)}, u32[]{:S(2)}) collective-permute-start(bf16[16,3072]{1,0:T(8,128)(2,1)S(1)} %get-tuple-element.53), channel_id=1, source_target_pairs={{0,2},{1,3},{2,0},{3,1},{4,6},{5,7},{6,4},{7,5},{8,10},{9,11},{10,... | collective-permute-start | bytes 294920 | tf_op jit(solution)/shard_map/ppermute | solution.py:313
  50.8 7.9 %collective-permute-start.18 = (bf16[16,3072]{1,0:T(8,128)(2,1)S(1)}, bf16[16,3072]{1,0:T(8,128)(2,1)S(1)}, u32[]{:S(2)}, u32[]{:S(2)}) collective-permute-start(bf16[16,3072]{1,0:T(8,128)(2,1)S(1)} %get-tuple-element.52), channel_id=1, source_target_pairs={{0,2},{1,3},{2,0},{3,1},{4,6},{5,7},{6,4},{7,5},{8,10},{9,11},{10,... | collective-permute-start | bytes 294920 | tf_op jit(solution)/shard_map/ppermute | solution.py:313
  53.1 7.6 %collective-permute-start.25 = (bf16[16,3072]{1,0:T(8,128)(2,1)S(1)}, bf16[16,3072]{1,0:T(8,128)(2,1)S(1)}, u32[]{:S(2)}, u32[]{:S(2)}) collective-permute-start(bf16[16,3072]{1,0:T(8,128)(2,1)S(1)} %shard_map.147), channel_id=1, source_target_pairs={{0,24},{1,29},{2,26},{3,31},{4,28},{5,25},{6,30},{7,27},{8,16},{9,... | collective-permute-start | bytes 294920 | tf_op jit(solution)/shard_map/ppermute | solution.py:321
  55.2 8.8 %collective-permute-start.23 = (bf16[16,3072]{1,0:T(8,128)(2,1)S(1)}, bf16[16,3072]{1,0:T(8,128)(2,1)S(1)}, u32[]{:S(2)}, u32[]{:S(2)}) collective-permute-start(bf16[16,3072]{1,0:T(8,128)(2,1)S(1)} %shard_map.146), channel_id=1, source_target_pairs={{0,16},{1,21},{2,18},{3,23},{4,20},{5,17},{6,22},{7,19},{8,24},{9,... | collective-permute-start | bytes 294920 | tf_op jit(solution)/shard_map/ppermute | solution.py:321
  57.8 6.3 %collective-permute-start.21 = (bf16[16,3072]{1,0:T(8,128)(2,1)S(1)}, bf16[16,3072]{1,0:T(8,128)(2,1)S(1)}, u32[]{:S(2)}, u32[]{:S(2)}) collective-permute-start(bf16[16,3072]{1,0:T(8,128)(2,1)S(1)} %shard_map.145), channel_id=1, source_target_pairs={{0,8},{1,13},{2,10},{3,15},{4,12},{5,9},{6,14},{7,11},{8,0},{9,5},... | collective-permute-start | bytes 294920 | tf_op jit(solution)/shard_map/ppermute | solution.py:321
  58.7 5.4 %collective-permute-start.19 = (bf16[16,3072]{1,0:T(8,128)(2,1)S(1)}, bf16[16,3072]{1,0:T(8,128)(2,1)S(1)}, u32[]{:S(2)}, u32[]{:S(2)}) collective-permute-start(bf16[16,3072]{1,0:T(8,128)(2,1)S(1)} %shard_map.144), channel_id=1, source_target_pairs={{0,0},{1,5},{2,2},{3,7},{4,4},{5,1},{6,6},{7,3},{8,8},{9,13},{10,1... | collective-permute-start | bytes 294920 | tf_op jit(solution)/shard_map/ppermute | solution.py:321
  64.6 3.5 %collective-permute-start.26 = (f32[32,1536]{1,0:T(8,128)S(1)}, f32[32,1536]{1,0:T(8,128)S(1)}, u32[]{:S(2)}, u32[]{:S(2)}) collective-permute-start(f32[32,1536]{1,0:T(8,128)S(1)} %get-tuple-element.57), channel_id=1, source_target_pairs={{0,1},{1,0},{2,3},{3,2},{4,5},{5,4},{6,7},{7,6},{8,9},{9,8},{10,11... | collective-permute-start | bytes 589832 | tf_op jit(solution)/shard_map/ppermute | solution.py:313
  (19 other events, 348.0 us)
